TPU v7x, 256 devices: a whole 4x4x8 slice. The times are simulated.
256 devices in a mesh: blk: 32 (over z, x_hi, core), col: 8 (over y, x_lo).
Axes of the slice: x: 4 (x_hi: 2, x_lo: 2; x = x_hi * 2 + x_lo), y: 4, z: 8, core: 2. Of those that a mesh axis runs over, the one named last changes fastest.
Arguments:
- targets: bfloat16 [32, 48, 72, 96], P('blk'), may hold values from -6 to 6
- sources: bfloat16 [512, 48, 72, 96], P(('blk', 'col')), may hold values from -6 to 6
- band_of_slot: int32 [512], P(('blk', 'col')), may hold values from 0 to 511, each once
- occupied: int32 [512], replicated, may hold values 0 or 1
Outputs:
- fock: float32 [32, 48, 72, 96], P('blk', 'col')
Inputs may be any that keep to these rules, and one draw needn't show every extreme that they name: `band_of_slot`: every band number appears in exactly one slot.
All inputs are finite; a program needn't handle non-finite values.
Results may differ from a plain program's by a relative error of at most 0.0003.
Values may be sent and summed in bfloat16 or wider, within the bound.
No kernel may reach another device: no remote copies, remote signals or barrier semaphores. Data moves between devices by JAX's collectives and lax.ppermute only.
A program may use at most 64 MiB of HBM per device.

v0:
```python
import math

import jax
import jax.numpy as jnp
import ml_dtypes
import numpy as np
from jax import lax
from jax.experimental import pallas as pl
from jax.experimental.pallas import tpu as pltpu
from jax.sharding import PartitionSpec as P

NX, NY, NZ = 48, 72, 96
LANES = 128
BASE = 36
TAIL = NX - BASE
HALF_Y = NY // 2 + 1
N_BLK, N_COL = 32, 8
SLICE = NX // N_COL
TILES = SLICE * NY // 8
KEPT = 41
SPARE = TILES - KEPT
AXES = ("blk", "col")
F32, BF16 = jnp.float32, jnp.bfloat16
grid_spacing = 0.3
screening = 0.11


def basis_of(length):
    row, col = np.arange(length)[:, None], np.arange(length)[None, :]
    angle = 2.0 * np.pi / length * (row * col % length)
    table = np.where(row <= length // 2, np.cos(angle), np.sin(angle))
    edge = (row == 0) | (row == length // 2)
    return table * np.where(edge, math.sqrt(1.0 / length), math.sqrt(2.0 / length))


def halves(table):
    high = table.astype(ml_dtypes.bfloat16)
    return high, (table - high.astype(np.float64)).astype(ml_dtypes.bfloat16)


def left_operand(table, pad):
    high, low = halves(table)
    gap = np.zeros((table.shape[0], pad), ml_dtypes.bfloat16)
    return np.concatenate([high, gap, high, gap, low, gap], axis=1)


def right_operand(table):
    size = table.shape[0]
    high, low = halves(table)
    out = np.zeros((2 * LANES, 2 * LANES), ml_dtypes.bfloat16)
    for row in (0, LANES):
        out[row : row + size, :size] = high
        out[row : row + size, LANES : LANES + size] = low
    return out


def frequency_sq(length):
    index = np.arange(length)
    return (2.0 * np.pi * np.minimum(index, length - index) / (length * grid_spacing)) ** 2


def kernel_field():
    g_sq = (
        frequency_sq(NY)[: HALF_Y, None, None]
        + frequency_sq(NX)[None, :, None]
        + frequency_sq(NZ)[None, None, :]
    )
    safe_sq = np.where(g_sq > 0, g_sq, 1.0)
    value = 4.0 * np.pi / safe_sq * (1.0 - np.exp(-safe_sq / (4.0 * screening * screening)))
    value = -0.125 * np.where(g_sq > 0, value, np.pi / (screening * screening))
    out = np.zeros((HALF_Y, NX, LANES), np.float32)
    out[:, :, :NZ] = value
    return out.reshape(HALF_Y * NX, LANES)


def constants():
    basis_x, basis_y, basis_z = basis_of(NX), basis_of(NY), basis_of(NZ)
    tables = (
        kernel_field(),
        left_operand(basis_y, 8),
        left_operand(basis_x, 0),
        right_operand(basis_z.T),
        right_operand(basis_z),
        left_operand(basis_x.T, 0),
        left_operand(basis_y.T, 8),
    )
    return tuple(jnp.asarray(table) for table in tables)


def dot(left, right):
    return jnp.dot(left, right, preferred_element_type=F32)


def split(value):
    high = value.astype(BF16)
    return high, (value - high.astype(F32)).astype(BF16)


def stacked(value):
    high, low = split(value)
    return jnp.concatenate([high, low, high], axis=0)


def stacked_y(value):
    return stacked(jnp.concatenate([value, jnp.zeros((8, LANES), F32)], axis=0))


def side(value):
    high, low = split(value)
    return jnp.concatenate([high, low], axis=1)


def folded(value):
    return value[:, :LANES] + value[:, LANES:]


def columns(value, which):
    return value[:, LANES * which : LANES * (which + 1)]


def widened(value):
    gap = jnp.zeros((value.shape[0], LANES - NZ), F32)
    return jnp.concatenate([value.astype(F32), gap], axis=1)


def lane_of(rows):
    return lax.broadcasted_iota(jnp.int32, (rows, LANES), 1)


def pack_kernel(band_ref, occupied_ref, source_ref, first_ref, second_ref, held, full, in_sems, out_sems):
    chunks = NX // TAIL
    planes = [pl.ds(chunk * TAIL, TAIL) for chunk in range(chunks)]
    order = [(slot, chunk) for slot in range(2) for chunk in (chunks - 1, *range(chunks - 1))]
    reads = {}
    for slot, chunk in order:
        reads[slot, chunk] = pltpu.make_async_copy(
            source_ref.at[slot, planes[chunk]], held.at[slot, planes[chunk]], in_sems.at[slot, chunk]
        )
        reads[slot, chunk].start()
    lane = lane_of(NY)
    writes = []
    for slot, out_ref in enumerate((first_ref, second_ref)):
        weight = jnp.where(occupied_ref[band_ref[slot]] > 0, 1.0, 0.0).astype(F32)
        reads[slot, chunks - 1].wait()
        for third in range(chunks - 1):
            reads[slot, third].wait()
            for index in range(TAIL):
                plane = third * TAIL + index
                base = widened(held[slot, plane])
                tail = pltpu.roll(widened(held[slot, BASE + index]), 96 - 32 * third, 1)
                full[slot, plane] = (jnp.where(lane < 96, base, tail) * weight).astype(BF16)
            write = pltpu.make_async_copy(
                full.at[slot, planes[third]], out_ref.at[planes[third]], out_sems.at[slot, third]
            )
            write.start()
            writes.append(write)
    for write in writes:
        write.wait()


def packed(sources, band_of_slot, occupied):
    anywhere = pl.BlockSpec(memory_space=pl.ANY)
    scalars = pl.BlockSpec(memory_space=pltpu.SMEM)
    shape = jax.ShapeDtypeStruct((BASE, NY, LANES), BF16)
    return pl.pallas_call(
        pack_kernel,
        out_shape=(shape, shape),
        in_specs=[scalars, scalars, anywhere],
        out_specs=(anywhere, anywhere),
        scratch_shapes=[
            pltpu.VMEM((2, NX, NY, NZ), BF16),
            pltpu.VMEM((2, BASE, NY, LANES), BF16),
            pltpu.SemaphoreType.DMA((2, NX // TAIL)),
            pltpu.SemaphoreType.DMA((2, BASE // TAIL)),
        ],
        compiler_params=pltpu.CompilerParams(vmem_limit_bytes=60 << 20),
        name="pack",
    )(band_of_slot, occupied, sources)


def solve_kernel(*refs, n_sources, has_accum, last):
    target_ref = refs[0]
    source_refs = refs[1 : 1 + n_sources]
    coulomb, left_y, left_x, right_z, right_k, left_p, left_q = refs[1 + n_sources : 8 + n_sources]
    rest = refs[8 + n_sources :]
    if has_accum:
        accum_in, rest = rest[0], rest[1:]
    out_ref, by_x, by_y, tail_ref, *more = rest
    accum = more[0] if last else out_ref

    lane = lane_of(NY)

    def held_plane(plane):
        return sum(ref[plane].astype(F32) for ref in source_refs)

    def first_plane(plane):
        if plane < BASE:
            return held_plane(plane)
        parts = [
            pltpu.roll(held_plane(plane - BASE + third * TAIL), 32 * third + 32, 1) for third in range(3)
        ]
        value = jnp.where(lane < 32, parts[0], jnp.where(lane < 64, parts[1], parts[2]))
        tail_ref[plane - BASE] = value.astype(BF16)
        return value

    def plane_of(plane):
        return held_plane(plane) if plane < BASE else tail_ref[plane - BASE].astype(F32)

    for plane in range(0, NX, 2):
        pair = [widened(target_ref[0, p]) * first_plane(p) for p in (plane, plane + 1)]
        spectrum = dot(left_y[...], jnp.concatenate([stacked_y(p) for p in pair], axis=1))
        for which in range(2):
            by_x[pl.ds(plane + which, NY, stride=NX), :] = columns(spectrum, which)

    group = 36

    def middle(step, carry):
        first = step * group
        rows = []
        for row in range(0, group, 2):
            lines = [
                by_x[pl.ds(pl.multiple_of((first + row + which) * NX, 8), NX), :] for which in range(2)
            ]
            spectrum = dot(left_x[...], jnp.concatenate([stacked(line) for line in lines], axis=1))
            rows += [side(columns(spectrum, which)) for which in range(2)]
        spectrum = folded(dot(jnp.concatenate(rows, axis=0), right_z[...]))
        field = []
        for row in range(group):
            freq = jnp.minimum(first + row, NY - first - row)
            field.append(coulomb[pl.ds(pl.multiple_of(freq * NX, 8), NX), :])
        spectrum = spectrum * jnp.concatenate(field, axis=0)
        field = folded(dot(side(spectrum), right_k[...]))
        for row in range(0, group, 2):
            lines = [field[(row + which) * NX : (row + which + 1) * NX] for which in range(2)]
            part = dot(left_p[...], jnp.concatenate([stacked(line) for line in lines], axis=1))
            for which in range(2):
                by_y[pl.ds(first + row + which, NX, stride=NY), :] = columns(part, which)
        return carry

    lax.fori_loop(0, NY // group, middle, 0)

    for plane in range(0, NX, 2):
        lines = [by_y[(plane + which) * NY : (plane + which + 1) * NY, :] for which in range(2)]
        potential = dot(left_q[...], jnp.concatenate([stacked_y(line) for line in lines], axis=1))
        for which in range(2):
            term = columns(potential, which) * plane_of(plane + which)
            if has_accum:
                term = term + accum_in[plane + which]
            accum[plane + which] = term

    if last:
        tile_lane = lane_of(8)

        def tile_of(piece, tile):
            plane, row = divmod(tile, NY // 8)
            return accum[piece * SLICE + plane, 8 * row : 8 * row + 8, :]

        def pack_slice(piece, carry):
            for tile in range(KEPT):
                value = tile_of(piece, tile)
                third, index = divmod(tile, SPARE)
                if third < 3:
                    spare = pltpu.roll(tile_of(piece, KEPT + index), 96 - 32 * third, 1)
                    value = jnp.where(tile_lane < 96, value, spare)
                out_ref[piece, 8 * tile : 8 * tile + 8, :] = value
            return carry

        lax.fori_loop(0, N_COL, pack_slice, 0)


def solved(target, source_list, tables, accum=None, last=False):
    whole = pl.BlockSpec(memory_space=pltpu.VMEM)
    operands = [target, *source_list, *tables] + ([accum] if accum is not None else [])
    scratch = [
        pltpu.VMEM((NX * NY, LANES), F32),
        pltpu.VMEM((NX * NY, LANES), F32),
        pltpu.VMEM((TAIL, NY, LANES), BF16),
    ]
    if last:
        shape = (N_COL, 8 * KEPT, LANES)
        scratch.append(pltpu.VMEM((NX, NY, LANES), F32))
    else:
        shape = (NX, NY, LANES)
    return pl.pallas_call(
        lambda *refs: solve_kernel(
            *refs, n_sources=len(source_list), has_accum=accum is not None, last=last
        ),
        out_shape=jax.ShapeDtypeStruct(shape, F32),
        in_specs=[whole] * len(operands),
        out_specs=whole,
        scratch_shapes=scratch,
        compiler_params=pltpu.CompilerParams(vmem_limit_bytes=40 << 20),
        cost_estimate=pl.CostEstimate(flops=2_000_000_000, bytes_accessed=4_000_000, transcendentals=0),
        name="solve",
    )(*operands)


def gather_kernel(parts_ref, out_ref, total_ref):
    lane = lane_of(8)
    for tile in range(KEPT):
        rows = slice(8 * tile, 8 * tile + 8)
        total = parts_ref[0, rows, :].astype(F32)
        for part in range(1, N_COL):
            total = total + parts_ref[part, rows, :].astype(F32)
        total_ref[rows, :] = total

    def put(tile, value):
        plane, row = divmod(tile, NY // 8)
        out_ref[0, plane, 8 * row : 8 * row + 8, :] = value[:, :NZ]

    for tile in range(KEPT):
        put(tile, total_ref[8 * tile : 8 * tile + 8, :])
    for index in range(SPARE):
        parts = []
        for third in range(3):
            tile = index + third * SPARE
            parts.append(pltpu.roll(total_ref[8 * tile : 8 * tile + 8, :], 32 * third + 32, 1))
        put(KEPT + index, jnp.where(lane < 32, parts[0], jnp.where(lane < 64, parts[1], parts[2])))


def gathered(parts):
    whole = pl.BlockSpec(memory_space=pltpu.VMEM)
    return pl.pallas_call(
        gather_kernel,
        out_shape=jax.ShapeDtypeStruct((1, SLICE, NY, NZ), F32),
        in_specs=[whole],
        out_specs=whole,
        scratch_shapes=[pltpu.VMEM((8 * KEPT, LANES), F32)],
        name="gather",
    )(parts)


def flat(block, col):
    return block % N_BLK * N_COL + col


def next_block():
    pairs = []
    for block in range(N_BLK):
        for col in range(N_COL):
            pairs.append((flat(block, col), flat(block + 1, col ^ (block % 2))))
    return pairs


def even_ahead():
    return [(flat(b, c), flat(b + 2, c ^ 1)) for b in range(0, N_BLK, 2) for c in range(N_COL)]


def even_to_odd():
    return [(flat(b, c), flat(b + 1, c)) for b in range(0, N_BLK, 2) for c in range(N_COL)]


def sent(value, pairs):
    return lax.ppermute(value, AXES, pairs)


def shards(targets, sources, band_of_slot, occupied):
    tables = constants()
    own = packed(sources, band_of_slot, occupied)
    near = [sent(own[slot], next_block()) for slot in range(2)]
    far = [sent(own[slot], even_ahead()) for slot in range(2)]
    passed = [sent(near[slot], even_to_odd()) for slot in range(2)]
    accum = solved(targets, [own[0]], tables)
    accum = solved(targets, [own[1]], tables, accum)
    accum = solved(targets, [near[0]], tables, accum)
    accum = solved(targets, [near[1]], tables, accum)
    accum = solved(targets, [far[0], passed[0]], tables, accum)
    pieces = solved(targets, [far[1], passed[1]], tables, accum, last=True)
    parts = lax.all_to_all(pieces, "col", 0, 0)
    return gathered(parts)


def solution(mesh):
    return jax.shard_map(
        shards,
        mesh=mesh,
        in_specs=(
            P("blk", None, None, None),
            P(("blk", "col"), None, None, None),
            P(("blk", "col")),
            P(),
        ),
        out_specs=P("blk", "col", None, None),
        check_vma=False,
    )
```

profile of v0, /device:TPU:224, one launch (start us, length us, event | category | flops | bytes accessed | tf_op | source)
XLA Modules:
  0.0 81.2 jit_solution(914354131682711207)
XLA Ops:
  0.0 0.0 copy-start.7
  0.0 0.0 copy-start.9
  0.0 0.0 copy-start.5
  0.0 0.0 copy-start.6
  0.0 0.0 copy-start.10
  0.0 0.0 copy-start.8
  0.0 0.0 copy-start
  0.1 3.5 %pack.1 = (bf16[36,72,128]{2,1,0:T(8,128)(2,1)}, bf16[36,72,128]{2,1,0:T(8,128)(2,1)}) custom-call(s32[2]{0:T(128)} %band_ref.1, s32[512]{0:T(512)} %occupied_ref.1, bf16[2,48,72,96]{3,2,1,0:T(8,128)(2,1)} %source_ref.1), custom_call_target="tpu_custom_call" | custom-call | tf_op jit(solution)/shard_map/pack/pallas_call | solution.py:165
  3.5 0.1 collective-permute-start.4
  3.6 0.0 copy-start.1
  3.6 2.9 %collective-permute-start.1 = (bf16[36,72,128]{2,1,0:T(8,128)(2,1)}, bf16[36,72,128]{2,1,0:T(8,128)(2,1)S(1)}, u32[]{:S(2)}, u32[]{:S(2)}) collective-permute-start(bf16[36,72,128]{2,1,0:T(8,128)(2,1)} %get-tuple-element.7.refs_1_), channel_id=1, source_target_pairs={{0,8},{1,9},{2,10},{3,11},{4,12},{5,13},{6,14},{7,15},{8,17},{9,16... | collective-permute-start | bytes 1990664 | tf_op jit(solution)/shard_map/ppermute | solution.py:354
  6.5 2.0 %collective-permute-start.3 = (bf16[36,72,128]{2,1,0:T(8,128)(2,1)}, bf16[36,72,128]{2,1,0:T(8,128)(2,1)S(1)}, u32[]{:S(2)}, u32[]{:S(2)}) collective-permute-start(bf16[36,72,128]{2,1,0:T(8,128)(2,1)} %get-tuple-element.8.refs_1_), channel_id=1, source_target_pairs={{0,17},{1,16},{2,19},{3,18},{4,21},{5,20},{6,23},{7,22},{16,33},{1... | collective-permute-start | bytes 1990664 | tf_op jit(solution)/shard_map/ppermute | solution.py:354
  8.5 1.9 %collective-permute-start = (bf16[36,72,128]{2,1,0:T(8,128)(2,1)}, bf16[36,72,128]{2,1,0:T(8,128)(2,1)S(1)}, u32[]{:S(2)}, u32[]{:S(2)}) collective-permute-start(bf16[36,72,128]{2,1,0:T(8,128)(2,1)} %get-tuple-element.7.refs_1_), channel_id=1, source_target_pairs={{0,17},{1,16},{2,19},{3,18},{4,21},{5,20},{6,23},{7,22},{16,33},{1... | collective-permute-start | bytes 1990664 | tf_op jit(solution)/shard_map/ppermute | solution.py:354
  10.5 7.3 %collective-permute-done.4.refs_1_ = bf16[36,72,128]{2,1,0:T(8,128)(2,1)S(1)} collective-permute-done((bf16[36,72,128]{2,1,0:T(8,128)(2,1)}, bf16[36,72,128]{2,1,0:T(8,128)(2,1)S(1)}, u32[]{:S(2)}, u32[]{:S(2)}) %collective-permute-start.4) | collective-permute-done | bytes 663584 | tf_op jit(solution)/shard_map/ppermute | solution.py:354
  17.8 2.9 %collective-permute-start.5 = (bf16[36,72,128]{2,1,0:T(8,128)(2,1)S(1)}, bf16[36,72,128]{2,1,0:T(8,128)(2,1)S(1)}, u32[]{:S(2)}, u32[]{:S(2)}) collective-permute-start(bf16[36,72,128]{2,1,0:T(8,128)(2,1)S(1)} %collective-permute-done.4.refs_1_), channel_id=1, source_target_pairs={{0,8},{1,9},{2,10},{3,11},{4,12},{5,13},{6,14},{7,15},{16,24},{17,... | collective-permute-start | bytes 1990664 | tf_op jit(solution)/shard_map/ppermute | solution.py:354
  20.8 0.0 copy-done.7
  20.8 0.0 copy-done.9
  20.8 0.0 copy-done.5
  20.8 0.0 copy-done.6
  20.8 0.0 copy-done.10
  20.8 0.0 copy-done.8
  20.8 0.0 copy-done
  20.8 0.0 copy-start.2
  20.8 1.1 %copy-done.2 = bf16[36,72,128]{2,1,0:T(8,128)(2,1)S(1)} copy-done((bf16[36,72,128]{2,1,0:T(8,128)(2,1)S(1)}, bf16[36,72,128]{2,1,0:T(8,128)(2,1)}, u32[]{:S(2)}) %copy-start.2) | copy-done | bytes 663576
  21.9 0.0 copy-start.3
  21.9 1.2 %copy-done.3 = f32[1776,128]{1,0:T(8,128)S(1)} copy-done((f32[1776,128]{1,0:T(8,128)S(1)}, f32[1776,128]{1,0:T(8,128)}, u32[]{:S(2)}) %copy-start.3) | copy-done | bytes 909336
  23.1 0.0 copy-start.4
  23.1 3.8 %solve.6.refs_9_ = f32[48,72,128]{2,1,0:T(8,128)S(1)} custom-call(bf16[1,48,72,96]{3,2,1,0:T(8,128)(2,1)S(1)} %copy-done, bf16[36,72,128]{2,1,0:T(8,128)(2,1)S(1)} %copy-done.2, f32[1776,128]{1,0:T(8,128)S(1)} %copy-done.3, bf16[72,240]{1,0:T(8,128)(2,1)S(1)} %copy-done.7, bf16[48,144]{1,0:T(8,128)(2,1)S(1)} %copy-done.9, bf16[256,256]{1,0:T(8,128)(2,1)S(1)} %copy-done.5, ...), custom_call_target="tpu_custom_call" | custom-call | flops 2000000000 | bytes 4000000 | tf_op jit(solution)/shard_map/solve/pallas_call | solution.py:284
  26.9 5.1 %collective-permute-done.1.refs_1_ = bf16[36,72,128]{2,1,0:T(8,128)(2,1)S(1)} collective-permute-done((bf16[36,72,128]{2,1,0:T(8,128)(2,1)}, bf16[36,72,128]{2,1,0:T(8,128)(2,1)S(1)}, u32[]{:S(2)}, u32[]{:S(2)}) %collective-permute-start.1) | collective-permute-done | bytes 663584 | tf_op jit(solution)/shard_map/ppermute | solution.py:354
  32.0 2.9 %collective-permute-start.2 = (bf16[36,72,128]{2,1,0:T(8,128)(2,1)S(1)}, bf16[36,72,128]{2,1,0:T(8,128)(2,1)S(1)}, u32[]{:S(2)}, u32[]{:S(2)}) collective-permute-start(bf16[36,72,128]{2,1,0:T(8,128)(2,1)S(1)} %collective-permute-done.1.refs_1_), channel_id=1, source_target_pairs={{0,8},{1,9},{2,10},{3,11},{4,12},{5,13},{6,14},{7,15},{16,24},{17,... | collective-permute-start | bytes 1990664 | tf_op jit(solution)/shard_map/ppermute | solution.py:354
  35.0 0.0 copy-done.1
  35.0 0.0 copy-done.4
  35.0 4.1 %solve.7.refs_9_ = f32[48,72,128]{2,1,0:T(8,128)S(1)} custom-call(bf16[1,48,72,96]{3,2,1,0:T(8,128)(2,1)S(1)} %copy-done, bf16[36,72,128]{2,1,0:T(8,128)(2,1)S(1)} %copy-done.1, f32[1776,128]{1,0:T(8,128)S(1)} %copy-done.4, bf16[72,240]{1,0:T(8,128)(2,1)S(1)} %copy-done.7, bf16[48,144]{1,0:T(8,128)(2,1)S(1)} %copy-done.9, bf16[256,256]{1,0:T(8,128)(2,1)S(1)} %copy-done.5, ...), custom_call_target="tpu_custom_call" | custom-call | flops 2000000000 | bytes 4000000 | tf_op jit(solution)/shard_map/solve/pallas_call | solution.py:284
  39.0 3.9 %solve.8.refs_9_ = f32[48,72,128]{2,1,0:T(8,128)S(1)} custom-call(bf16[1,48,72,96]{3,2,1,0:T(8,128)(2,1)S(1)} %copy-done, bf16[36,72,128]{2,1,0:T(8,128)(2,1)S(1)} %collective-permute-done.4.refs_1_, f32[1776,128]{1,0:T(8,128)S(1)} %copy-done.4, bf16[72,240]{1,0:T(8,128)(2,1)S(1)} %copy-done.7, bf16[48,144]{1,0:T(8,128)(2,1)S(1)} %copy-done.9, ...), custom_call_target="tpu_custom_call" | custom-call | flops 2000000000 | bytes 4000000 | tf_op jit(solution)/shard_map/solve/pallas_call | solution.py:284
  42.9 3.9 %solve.9.refs_10_ = f32[48,72,128]{2,1,0:T(8,128)S(1)} custom-call(bf16[1,48,72,96]{3,2,1,0:T(8,128)(2,1)S(1)} %copy-done, bf16[36,72,128]{2,1,0:T(8,128)(2,1)S(1)} %collective-permute-done.1.refs_1_, f32[1776,128]{1,0:T(8,128)S(1)} %copy-done.4, bf16[72,240]{1,0:T(8,128)(2,1)S(1)} %copy-done.7, bf16[48,144]{1,0:T(8,128)(2,1)S(1)} %copy-done.9, ...), custom_call_target="tpu_custom_call" | custom-call | flops 2000000000 | bytes 4000000 | tf_op jit(solution)/shard_map/solve/pallas_call | solution.py:284
  46.8 0.0 collective-permute-done.3.refs_1_
  46.8 0.0 collective-permute-done.5.refs_2_
  46.9 4.2 %solve.10.refs_10_ = f32[48,72,128]{2,1,0:T(8,128)S(1)} custom-call(bf16[1,48,72,96]{3,2,1,0:T(8,128)(2,1)S(1)} %copy-done, bf16[36,72,128]{2,1,0:T(8,128)(2,1)S(1)} %collective-permute-done.3.refs_1_, bf16[36,72,128]{2,1,0:T(8,128)(2,1)S(1)} %collective-permute-done.5.refs_2_, f32[1776,128]{1,0:T(8,128)S(1)} %copy-done.4, bf16[72,240]{1,0:T(8,128)(2,1)S(1)} %copy-done.7, ...), custom_call_target="tpu_custom_call" | custom-call | flops 2000000000 | bytes 4000000 | tf_op jit(solution)/shard_map/solve/pallas_call | solution.py:284
  51.0 0.0 collective-permute-done.refs_1_
  51.0 0.0 collective-permute-done.2.refs_2_
  51.0 5.0 %solve.11 = f32[8,328,128]{2,1,0:T(8,128)S(1)} custom-call(bf16[1,48,72,96]{3,2,1,0:T(8,128)(2,1)S(1)} %copy-done, bf16[36,72,128]{2,1,0:T(8,128)(2,1)S(1)} %collective-permute-done.refs_1_, bf16[36,72,128]{2,1,0:T(8,128)(2,1)S(1)} %collective-permute-done.2.refs_2_, f32[1776,128]{1,0:T(8,128)S(1)} %copy-done.4, bf16[72,240]{1,0:T(8,128)(2,1)S(1)} %copy-done.7, ...), custom_call_target="tpu_custom_call" | custom-call | flops 2000000000 | bytes 4000000 | tf_op jit(solution)/shard_map/solve/pallas_call | solution.py:284
  56.1 22.9 %all_to_all.5.parts_ref = f32[8,328,128]{2,1,0:T(8,128)} all-to-all(f32[8,328,128]{2,1,0:T(8,128)S(1)} %solve.11), channel_id=1, replica_groups=mesh['blk'=32,'col'=8] {'col'}, dimensions={0} | all-to-all | bytes 2686976 | tf_op jit(solution)/shard_map/all_to_all | solution.py:369
  79.0 2.1 %gather.1 = f32[1,6,72,96]{3,2,1,0:T(8,128)} custom-call(f32[8,328,128]{2,1,0:T(8,128)} %all_to_all.5.parts_ref), custom_call_target="tpu_custom_call" | custom-call | tf_op jit(solution)/shard_map/gather/pallas_call | solution.py:323
Async XLA Ops:
  0.0 20.8 %copy-start.7 = (bf16[72,240]{1,0:T(8,128)(2,1)S(1)}, bf16[72,240]{1,0:T(8,128)(2,1)}, u32[]{:S(2)}) copy-start(bf16[72,240]{1,0:T(8,128)(2,1)} %constant.15.clone.refs_3_.refs_4_) | copy-start | bytes 103684
  0.0 20.8 %copy-start.9 = (bf16[48,144]{1,0:T(8,128)(2,1)S(1)}, bf16[48,144]{1,0:T(8,128)(2,1)}, u32[]{:S(2)}) copy-start(bf16[48,144]{1,0:T(8,128)(2,1)} %constant.16.clone.refs_4_.refs_5_) | copy-start | bytes 41476
  0.0 20.8 %copy-start.5 = (bf16[256,256]{1,0:T(8,128)(2,1)S(1)}, bf16[256,256]{1,0:T(8,128)(2,1)}, u32[]{:S(2)}) copy-start(bf16[256,256]{1,0:T(8,128)(2,1)} %constant.17.clone.refs_5_.refs_6_) | copy-start | bytes 393220
  0.0 20.8 %copy-start.6 = (bf16[256,256]{1,0:T(8,128)(2,1)S(1)}, bf16[256,256]{1,0:T(8,128)(2,1)}, u32[]{:S(2)}) copy-start(bf16[256,256]{1,0:T(8,128)(2,1)} %constant.18.clone.refs_6_.refs_7_) | copy-start | bytes 393220
  0.0 20.8 %copy-start.10 = (bf16[48,144]{1,0:T(8,128)(2,1)S(1)}, bf16[48,144]{1,0:T(8,128)(2,1)}, u32[]{:S(2)}) copy-start(bf16[48,144]{1,0:T(8,128)(2,1)} %constant.19.clone.refs_7_.refs_8_) | copy-start | bytes 41476
  0.0 20.8 %copy-start.8 = (bf16[72,240]{1,0:T(8,128)(2,1)S(1)}, bf16[72,240]{1,0:T(8,128)(2,1)}, u32[]{:S(2)}) copy-start(bf16[72,240]{1,0:T(8,128)(2,1)} %constant.20.clone.refs_8_.refs_9_) | copy-start | bytes 103684
  0.0 20.8 %copy-start = (bf16[1,48,72,96]{3,2,1,0:T(8,128)(2,1)S(1)}, bf16[1,48,72,96]{3,2,1,0:T(8,128)(2,1)}, u32[]{:S(2)}) copy-start(bf16[1,48,72,96]{3,2,1,0:T(8,128)(2,1)} %refs_0_.11) | copy-start | bytes 1990660
  3.5 14.3 %collective-permute-start.4 = (bf16[36,72,128]{2,1,0:T(8,128)(2,1)}, bf16[36,72,128]{2,1,0:T(8,128)(2,1)S(1)}, u32[]{:S(2)}, u32[]{:S(2)}) collective-permute-start(bf16[36,72,128]{2,1,0:T(8,128)(2,1)} %get-tuple-element.8.refs_1_), channel_id=1, source_target_pairs={{0,8},{1,9},{2,10},{3,11},{4,12},{5,13},{6,14},{7,15},{8,17},{9,16... | collective-permute-start | bytes 1990664 | tf_op jit(solution)/shard_map/ppermute | solution.py:354
  3.6 31.4 %copy-start.1 = (bf16[36,72,128]{2,1,0:T(8,128)(2,1)S(1)}, bf16[36,72,128]{2,1,0:T(8,128)(2,1)}, u32[]{:S(2)}) copy-start(bf16[36,72,128]{2,1,0:T(8,128)(2,1)} %get-tuple-element.7.refs_1_) | copy-start | bytes 1990660
  3.6 28.4 %collective-permute-start.1 = (bf16[36,72,128]{2,1,0:T(8,128)(2,1)}, bf16[36,72,128]{2,1,0:T(8,128)(2,1)S(1)}, u32[]{:S(2)}, u32[]{:S(2)}) collective-permute-start(bf16[36,72,128]{2,1,0:T(8,128)(2,1)} %get-tuple-element.7.refs_1_), channel_id=1, source_target_pairs={{0,8},{1,9},{2,10},{3,11},{4,12},{5,13},{6,14},{7,15},{8,17},{9,16... | collective-permute-start | bytes 1990664 | tf_op jit(solution)/shard_map/ppermute | solution.py:354
  6.5 40.3 %collective-permute-start.3 = (bf16[36,72,128]{2,1,0:T(8,128)(2,1)}, bf16[36,72,128]{2,1,0:T(8,128)(2,1)S(1)}, u32[]{:S(2)}, u32[]{:S(2)}) collective-permute-start(bf16[36,72,128]{2,1,0:T(8,128)(2,1)} %get-tuple-element.8.refs_1_), channel_id=1, source_target_pairs={{0,17},{1,16},{2,19},{3,18},{4,21},{5,20},{6,23},{7,22},{16,33},{1... | collective-permute-start | bytes 1990664 | tf_op jit(solution)/shard_map/ppermute | solution.py:354
  8.5 42.5 %collective-permute-start = (bf16[36,72,128]{2,1,0:T(8,128)(2,1)}, bf16[36,72,128]{2,1,0:T(8,128)(2,1)S(1)}, u32[]{:S(2)}, u32[]{:S(2)}) collective-permute-start(bf16[36,72,128]{2,1,0:T(8,128)(2,1)} %get-tuple-element.7.refs_1_), channel_id=1, source_target_pairs={{0,17},{1,16},{2,19},{3,18},{4,21},{5,20},{6,23},{7,22},{16,33},{1... | collective-permute-start | bytes 1990664 | tf_op jit(solution)/shard_map/ppermute | solution.py:354
  17.8 29.0 %collective-permute-start.5 = (bf16[36,72,128]{2,1,0:T(8,128)(2,1)S(1)}, bf16[36,72,128]{2,1,0:T(8,128)(2,1)S(1)}, u32[]{:S(2)}, u32[]{:S(2)}) collective-permute-start(bf16[36,72,128]{2,1,0:T(8,128)(2,1)S(1)} %collective-permute-done.4.refs_1_), channel_id=1, source_target_pairs={{0,8},{1,9},{2,10},{3,11},{4,12},{5,13},{6,14},{7,15},{16,24},{17,... | collective-permute-start | bytes 1990664 | tf_op jit(solution)/shard_map/ppermute | solution.py:354
  20.8 1.1 %copy-start.2 = (bf16[36,72,128]{2,1,0:T(8,128)(2,1)S(1)}, bf16[36,72,128]{2,1,0:T(8,128)(2,1)}, u32[]{:S(2)}) copy-start(bf16[36,72,128]{2,1,0:T(8,128)(2,1)} %get-tuple-element.8.refs_1_) | copy-start | bytes 1990660
  21.9 1.2 %copy-start.3 = (f32[1776,128]{1,0:T(8,128)S(1)}, f32[1776,128]{1,0:T(8,128)}, u32[]{:S(2)}) copy-start(f32[1776,128]{1,0:T(8,128)} %constant.14.clone.refs_2_.refs_3_) | copy-start | bytes 2727940
  23.1 11.9 %copy-start.4 = (f32[1776,128]{1,0:T(8,128)S(1)}, f32[1776,128]{1,0:T(8,128)}, u32[]{:S(2)}) copy-start(f32[1776,128]{1,0:T(8,128)} %constant.14.clone.refs_2_.refs_3_) | copy-start | bytes 2727940
  32.0 19.0 %collective-permute-start.2 = (bf16[36,72,128]{2,1,0:T(8,128)(2,1)S(1)}, bf16[36,72,128]{2,1,0:T(8,128)(2,1)S(1)}, u32[]{:S(2)}, u32[]{:S(2)}) collective-permute-start(bf16[36,72,128]{2,1,0:T(8,128)(2,1)S(1)} %collective-permute-done.1.refs_1_), channel_id=1, source_target_pairs={{0,8},{1,9},{2,10},{3,11},{4,12},{5,13},{6,14},{7,15},{16,24},{17,... | collective-permute-start | bytes 1990664 | tf_op jit(solution)/shard_map/ppermute | solution.py:354
where the time goes:
time: 81.5 us; the launch traced here: 81.2 us
  Pallas kernels  30.5 us (37%)
  blocking collectives  22.9 us (28%)
  starting transfers between devices  12.8 us (16%)
  waiting for transfers between devices  12.4 us (15%)
  local copies, waits for them, and re-layouts  2.3 us (3%)
    pallas_call x6, Pallas kernels, solved(): pl.pallas_call(lambda *refs: solve_kernel(*refs, n_sources=len(source_lis...  24.9 us
    all_to_all x1, blocking collectives, shards(): parts = lax.all_to_all(pieces, 'col', 0, 0)  22.9 us
    ppermute x6, starting transfers between devices, sent(): return lax.ppermute(value, AXES, pairs)  12.8 us
    ppermute x6, waiting for transfers between devices, sent(): return lax.ppermute(value, AXES, pairs)  12.4 us
    pallas_call x1, Pallas kernels, packed(): pl.pallas_call(pack_kernel, out_shape=(shape, shape), in_specs=[scalars,...  3.47 us
    unnamed x22, local copies, waits for them, and re-layouts  2.3 us
    pallas_call x1, Pallas kernels, gathered(): pl.pallas_call(gather_kernel, out_shape=jax.ShapeDtypeStruct((1, SLICE, N...  2.14 us
  transfers between devices with their start and end apart: 6, of which 2 were waited for; matrix products, arithmetic and copies ran while one was open for 0% of the time, Pallas kernels for 24%

commit v1 on v0

--- a/solution.py
+++ b/solution.py
@@ -127,7 +127,11 @@
     return lax.broadcasted_iota(jnp.int32, (rows, LANES), 1)
 
 
-def pack_kernel(band_ref, occupied_ref, source_ref, first_ref, second_ref, held, full, in_sems, out_sems):
+def in_hbm(value):
+    return pltpu.with_memory_space_constraint(value, pltpu.HBM)
+
+
+def pack_kernel(band_ref, occupied_ref, source_ref, first_ref, second_ref, held, in_sems):
     chunks = NX // TAIL
     planes = [pl.ds(chunk * TAIL, TAIL) for chunk in range(chunks)]
     order = [(slot, chunk) for slot in range(2) for chunk in (chunks - 1, *range(chunks - 1))]
@@ -138,7 +142,6 @@
         )
         reads[slot, chunk].start()
     lane = lane_of(NY)
-    writes = []
     for slot, out_ref in enumerate((first_ref, second_ref)):
         weight = jnp.where(occupied_ref[band_ref[slot]] > 0, 1.0, 0.0).astype(F32)
         reads[slot, chunks - 1].wait()
@@ -148,34 +151,49 @@
                 plane = third * TAIL + index
                 base = widened(held[slot, plane])
                 tail = pltpu.roll(widened(held[slot, BASE + index]), 96 - 32 * third, 1)
-                full[slot, plane] = (jnp.where(lane < 96, base, tail) * weight).astype(BF16)
-            write = pltpu.make_async_copy(
-                full.at[slot, planes[third]], out_ref.at[planes[third]], out_sems.at[slot, third]
-            )
-            write.start()
-            writes.append(write)
-    for write in writes:
-        write.wait()
+                out_ref[plane] = (jnp.where(lane < 96, base, tail) * weight).astype(BF16)
 
 
 def packed(sources, band_of_slot, occupied):
     anywhere = pl.BlockSpec(memory_space=pl.ANY)
+    whole = pl.BlockSpec(memory_space=pltpu.VMEM)
     scalars = pl.BlockSpec(memory_space=pltpu.SMEM)
     shape = jax.ShapeDtypeStruct((BASE, NY, LANES), BF16)
     return pl.pallas_call(
         pack_kernel,
         out_shape=(shape, shape),
         in_specs=[scalars, scalars, anywhere],
-        out_specs=(anywhere, anywhere),
+        out_specs=(whole, whole),
         scratch_shapes=[
             pltpu.VMEM((2, NX, NY, NZ), BF16),
-            pltpu.VMEM((2, BASE, NY, LANES), BF16),
             pltpu.SemaphoreType.DMA((2, NX // TAIL)),
-            pltpu.SemaphoreType.DMA((2, BASE // TAIL)),
         ],
-        compiler_params=pltpu.CompilerParams(vmem_limit_bytes=60 << 20),
+        compiler_params=pltpu.CompilerParams(vmem_limit_bytes=16 << 20),
         name="pack",
-    )(band_of_slot, occupied, sources)
+    )(*(in_hbm(value) for value in (band_of_slot, occupied, sources)))
+
+
+def store_piece(accum, out_ref, piece):
+    lane = lane_of(8)
+
+    def tile_of(tile):
+        plane, row = divmod(tile, NY // 8)
+        return accum[piece * SLICE + plane, 8 * row : 8 * row + 8, :]
+
+    largest = jnp.abs(tile_of(0))
+    for tile in range(1, TILES):
+        largest = jnp.maximum(largest, jnp.abs(tile_of(tile)))
+    largest = jnp.max(largest, axis=(0, 1), keepdims=True)
+    shift = jnp.floor(jnp.log2(jnp.maximum(largest, 1e-30))) - 14.0
+    factor = jnp.broadcast_to(jnp.exp2(-shift), (8, LANES))
+    spare = [tile_of(KEPT + index) * factor for index in range(SPARE)]
+    for tile in range(KEPT):
+        value = tile_of(tile) * factor
+        third, index = divmod(tile, SPARE)
+        if third < 3:
+            value = jnp.where(lane < 96, value, pltpu.roll(spare[index], 96 - 32 * third, 1))
+        out_ref[piece, 8 * tile : 8 * tile + 8, :] = value
+    out_ref[piece, 8 * KEPT :, :] = jnp.broadcast_to(shift, (8, LANES))
 
 
 def solve_kernel(*refs, n_sources, has_accum, last):
@@ -185,7 +203,14 @@
     rest = refs[8 + n_sources :]
     if has_accum:
         accum_in, rest = rest[0], rest[1:]
+    if not has_accum:
+        wide_ref, held_coulomb, *others = rest[1:]
+        rest = (rest[0], *others)
     out_ref, by_x, by_y, tail_ref, *more = rest
+    if not has_accum:
+        fetch = pltpu.make_async_copy(coulomb, held_coulomb, more[0])
+        fetch.start()
+        coulomb = held_coulomb
     accum = more[0] if last else out_ref
 
     lane = lane_of(NY)
@@ -206,20 +231,29 @@
     def plane_of(plane):
         return held_plane(plane) if plane < BASE else tail_ref[plane - BASE].astype(F32)
 
+    def target_plane(plane):
+        if has_accum:
+            return target_ref[plane].astype(F32)
+        value = widened(target_ref[0, plane])
+        wide_ref[plane] = value.astype(BF16)
+        return value
+
     for plane in range(0, NX, 2):
-        pair = [widened(target_ref[0, p]) * first_plane(p) for p in (plane, plane + 1)]
+        pair = [target_plane(p) * first_plane(p) for p in (plane, plane + 1)]
         spectrum = dot(left_y[...], jnp.concatenate([stacked_y(p) for p in pair], axis=1))
         for which in range(2):
-            by_x[pl.ds(plane + which, NY, stride=NX), :] = columns(spectrum, which)
-
-    group = 36
+            by_x[(plane + which) * NY : (plane + which + 1) * NY, :] = columns(spectrum, which)
+
+    if not has_accum:
+        fetch.wait()
+    group = NY if has_accum else NY // 2
 
     def middle(step, carry):
         first = step * group
         rows = []
         for row in range(0, group, 2):
             lines = [
-                by_x[pl.ds(pl.multiple_of((first + row + which) * NX, 8), NX), :] for which in range(2)
+                by_x[pl.ds(first + row + which, NX, stride=NY), :] for which in range(2)
             ]
             spectrum = dot(left_x[...], jnp.concatenate([stacked(line) for line in lines], axis=1))
             rows += [side(columns(spectrum, which)) for which in range(2)]
@@ -247,25 +281,8 @@
             if has_accum:
                 term = term + accum_in[plane + which]
             accum[plane + which] = term
-
-    if last:
-        tile_lane = lane_of(8)
-
-        def tile_of(piece, tile):
-            plane, row = divmod(tile, NY // 8)
-            return accum[piece * SLICE + plane, 8 * row : 8 * row + 8, :]
-
-        def pack_slice(piece, carry):
-            for tile in range(KEPT):
-                value = tile_of(piece, tile)
-                third, index = divmod(tile, SPARE)
-                if third < 3:
-                    spare = pltpu.roll(tile_of(piece, KEPT + index), 96 - 32 * third, 1)
-                    value = jnp.where(tile_lane < 96, value, spare)
-                out_ref[piece, 8 * tile : 8 * tile + 8, :] = value
-            return carry
-
-        lax.fori_loop(0, N_COL, pack_slice, 0)
+        if last and (plane + 2) % SLICE == 0:
+            store_piece(accum, out_ref, plane // SLICE)
 
 
 def solved(target, source_list, tables, accum=None, last=False):
@@ -277,17 +294,25 @@
         pltpu.VMEM((TAIL, NY, LANES), BF16),
     ]
     if last:
-        shape = (N_COL, 8 * KEPT, LANES)
+        shape = (N_COL, 8 * KEPT + 8, LANES)
         scratch.append(pltpu.VMEM((NX, NY, LANES), F32))
     else:
         shape = (NX, NY, LANES)
+    out_shape = [jax.ShapeDtypeStruct(shape, F32)]
+    if accum is None:
+        out_shape.append(jax.ShapeDtypeStruct((NX, NY, LANES), BF16))
+        out_shape.append(jax.ShapeDtypeStruct((HALF_Y * NX, LANES), F32))
+        scratch.append(pltpu.SemaphoreType.DMA)
     return pl.pallas_call(
         lambda *refs: solve_kernel(
             *refs, n_sources=len(source_list), has_accum=accum is not None, last=last
         ),
-        out_shape=jax.ShapeDtypeStruct(shape, F32),
-        in_specs=[whole] * len(operands),
-        out_specs=whole,
+        out_shape=out_shape,
+        in_specs=[
+            pl.BlockSpec(memory_space=pl.ANY) if accum is None and index == 2 else whole
+            for index in range(len(operands))
+        ],
+        out_specs=[whole] * len(out_shape),
         scratch_shapes=scratch,
         compiler_params=pltpu.CompilerParams(vmem_limit_bytes=40 << 20),
         cost_estimate=pl.CostEstimate(flops=2_000_000_000, bytes_accessed=4_000_000, transcendentals=0),
@@ -295,14 +320,8 @@
     )(*operands)
 
 
-def gather_kernel(parts_ref, out_ref, total_ref):
+def gather_kernel(total_ref, out_ref):
     lane = lane_of(8)
-    for tile in range(KEPT):
-        rows = slice(8 * tile, 8 * tile + 8)
-        total = parts_ref[0, rows, :].astype(F32)
-        for part in range(1, N_COL):
-            total = total + parts_ref[part, rows, :].astype(F32)
-        total_ref[rows, :] = total
 
     def put(tile, value):
         plane, row = divmod(tile, NY // 8)
@@ -320,14 +339,16 @@
 
 def gathered(parts):
     whole = pl.BlockSpec(memory_space=pltpu.VMEM)
+    wide = parts.astype(F32)
+    total = jnp.sum(wide[:, : 8 * KEPT] * jnp.exp2(wide[:, 8 * KEPT : 8 * KEPT + 1, :1]), axis=0)
     return pl.pallas_call(
         gather_kernel,
         out_shape=jax.ShapeDtypeStruct((1, SLICE, NY, NZ), F32),
         in_specs=[whole],
         out_specs=whole,
-        scratch_shapes=[pltpu.VMEM((8 * KEPT, LANES), F32)],
+        compiler_params=pltpu.CompilerParams(vmem_limit_bytes=16 << 20),
         name="gather",
-    )(parts)
+    )(total)
 
 
 def flat(block, col):
@@ -360,13 +381,14 @@
     near = [sent(own[slot], next_block()) for slot in range(2)]
     far = [sent(own[slot], even_ahead()) for slot in range(2)]
     passed = [sent(near[slot], even_to_odd()) for slot in range(2)]
-    accum = solved(targets, [own[0]], tables)
-    accum = solved(targets, [own[1]], tables, accum)
-    accum = solved(targets, [near[0]], tables, accum)
-    accum = solved(targets, [near[1]], tables, accum)
-    accum = solved(targets, [far[0], passed[0]], tables, accum)
-    pieces = solved(targets, [far[1], passed[1]], tables, accum, last=True)
-    parts = lax.all_to_all(pieces, "col", 0, 0)
+    accum, target, coulomb = solved(targets, [own[0]], (in_hbm(tables[0]), *tables[1:]))
+    tables = (coulomb, *tables[1:])
+    (accum,) = solved(target, [own[1]], tables, accum)
+    (accum,) = solved(target, [near[0]], tables, accum)
+    (accum,) = solved(target, [near[1]], tables, accum)
+    (accum,) = solved(target, [far[0], passed[0]], tables, accum)
+    (pieces,) = solved(target, [far[1], passed[1]], tables, accum, last=True)
+    parts = lax.all_to_all(pieces.astype(jnp.float16), "col", 0, 0)
     return gathered(parts)
 
 

time: 81.5 us -> 72.2 us (0.89)
  the two profiles are of different devices: /device:TPU:224 before, /device:TPU:2 now
where the time goes in v1:
time: 72.2 us; the launch traced here: 71.9 us
  Pallas kernels  26.2 us (36%)
  waiting for transfers between devices  18.8 us (26%)
  blocking collectives  14.4 us (20%)
  starting transfers between devices  11.7 us (16%)
    pallas_call x6, Pallas kernels, solved(): pl.pallas_call(lambda *refs: solve_kernel(*refs, n_sources=len(source_lis...  22.7 us
    ppermute x6, waiting for transfers between devices, sent(): return lax.ppermute(value, AXES, pairs)  18.8 us
    all_to_all x1, blocking collectives, shards(): parts = lax.all_to_all(pieces.astype(jnp.float16), 'col', 0, 0)  14.4 us
    ppermute x6, starting transfers between devices, sent(): return lax.ppermute(value, AXES, pairs)  11.7 us
    pallas_call x1, Pallas kernels, packed(): pl.pallas_call(pack_kernel, out_shape=(shape, shape), in_specs=[scalars,...  2.73 us
  transfers between devices with their start and end apart: 6, of which 2 were waited for; matrix products, arithmetic and copies ran while one was open for 0% of the time, Pallas kernels for 26%

profile of v1, /device:TPU:2, one launch (start us, length us, event | category | flops | bytes accessed | tf_op | source)
XLA Modules:
  0.0 71.9 jit_solution(3674586275329158073)
XLA Ops:
  0.0 0.0 copy-start.3
  0.0 0.0 copy-start.5
  0.0 0.0 copy-start.1
  0.0 0.0 copy-start.2
  0.0 0.0 copy-start.6
  0.0 0.0 copy-start.4
  0.0 0.0 copy-start
  0.1 2.7 %pack.1 = (bf16[36,72,128]{2,1,0:T(8,128)(2,1)S(1)}, bf16[36,72,128]{2,1,0:T(8,128)(2,1)S(1)}) custom-call(s32[2]{0:T(128)} %band_ref.1, s32[512]{0:T(512)} %occupied_ref.1, bf16[2,48,72,96]{3,2,1,0:T(8,128)(2,1)} %source_ref.1), custom_call_target="tpu_custom_call" | custom-call | tf_op jit(solution)/shard_map/pack/pallas_call | solution.py:162
  2.8 0.1 collective-permute-start.4
  2.9 1.6 %collective-permute-start.1 = (bf16[36,72,128]{2,1,0:T(8,128)(2,1)S(1)}, bf16[36,72,128]{2,1,0:T(8,128)(2,1)S(1)}, u32[]{:S(2)}, u32[]{:S(2)}) collective-permute-start(bf16[36,72,128]{2,1,0:T(8,128)(2,1)S(1)} %get-tuple-element.12.refs_1_), channel_id=1, source_target_pairs={{0,8},{1,9},{2,10},{3,11},{4,12},{5,13},{6,14},{7,15},{8,17},{9,16... | collective-permute-start | bytes 1990664 | tf_op jit(solution)/shard_map/ppermute | solution.py:375
  4.5 3.8 %collective-permute-start.3 = (bf16[36,72,128]{2,1,0:T(8,128)(2,1)S(1)}, bf16[36,72,128]{2,1,0:T(8,128)(2,1)S(1)}, u32[]{:S(2)}, u32[]{:S(2)}) collective-permute-start(bf16[36,72,128]{2,1,0:T(8,128)(2,1)S(1)} %get-tuple-element.10.refs_1_), channel_id=1, source_target_pairs={{0,17},{1,16},{2,19},{3,18},{4,21},{5,20},{6,23},{7,22},{16,33},{1... | collective-permute-start | bytes 1990664 | tf_op jit(solution)/shard_map/ppermute | solution.py:375
  8.3 3.4 %collective-permute-start = (bf16[36,72,128]{2,1,0:T(8,128)(2,1)S(1)}, bf16[36,72,128]{2,1,0:T(8,128)(2,1)S(1)}, u32[]{:S(2)}, u32[]{:S(2)}) collective-permute-start(bf16[36,72,128]{2,1,0:T(8,128)(2,1)S(1)} %get-tuple-element.12.refs_1_), channel_id=1, source_target_pairs={{0,17},{1,16},{2,19},{3,18},{4,21},{5,20},{6,23},{7,22},{16,33},{1... | collective-permute-start | bytes 1990664 | tf_op jit(solution)/shard_map/ppermute | solution.py:375
  11.7 10.0 %collective-permute-done.4.refs_1_ = bf16[36,72,128]{2,1,0:T(8,128)(2,1)S(1)} collective-permute-done((bf16[36,72,128]{2,1,0:T(8,128)(2,1)S(1)}, bf16[36,72,128]{2,1,0:T(8,128)(2,1)S(1)}, u32[]{:S(2)}, u32[]{:S(2)}) %collective-permute-start.4) | collective-permute-done | bytes 663584 | tf_op jit(solution)/shard_map/ppermute | solution.py:375
  21.7 1.3 %collective-permute-start.5 = (bf16[36,72,128]{2,1,0:T(8,128)(2,1)S(1)}, bf16[36,72,128]{2,1,0:T(8,128)(2,1)S(1)}, u32[]{:S(2)}, u32[]{:S(2)}) collective-permute-start(bf16[36,72,128]{2,1,0:T(8,128)(2,1)S(1)} %collective-permute-done.4.refs_1_), channel_id=1, source_target_pairs={{0,8},{1,9},{2,10},{3,11},{4,12},{5,13},{6,14},{7,15},{16,24},{17,... | collective-permute-start | bytes 1990664 | tf_op jit(solution)/shard_map/ppermute | solution.py:375
  23.0 0.0 copy-done.3
  23.0 0.0 copy-done.5
  23.0 0.0 copy-done.1
  23.1 0.0 copy-done.2
  23.1 0.0 copy-done.6
  23.1 0.0 copy-done.4
  23.1 0.0 copy-done
  23.1 4.0 %solve.6 = (f32[48,72,128]{2,1,0:T(8,128)S(1)}, bf16[48,72,128]{2,1,0:T(8,128)(2,1)S(1)}, f32[1776,128]{1,0:T(8,128)S(1)}) custom-call(bf16[1,48,72,96]{3,2,1,0:T(8,128)(2,1)S(1)} %copy-done, bf16[36,72,128]{2,1,0:T(8,128)(2,1)S(1)} %get-tuple-element.10.refs_1_, f32[1776,128]{1,0:T(8,128)} %constant.18.clone.refs_2_, bf16[72,240]{1,0:T(8,128)(2,1)S(1)} %copy-done.3, ...), custom_call_target="tpu_custom_call" | custom-call | flops 2000000000 | bytes 4000000 | tf_op jit(solution)/shard_map/solve/pallas_call | solution.py:306
  27.1 8.8 %collective-permute-done.1.refs_1_ = bf16[36,72,128]{2,1,0:T(8,128)(2,1)S(1)} collective-permute-done((bf16[36,72,128]{2,1,0:T(8,128)(2,1)S(1)}, bf16[36,72,128]{2,1,0:T(8,128)(2,1)S(1)}, u32[]{:S(2)}, u32[]{:S(2)}) %collective-permute-start.1) | collective-permute-done | bytes 663584 | tf_op jit(solution)/shard_map/ppermute | solution.py:375
  35.9 1.5 %collective-permute-start.2 = (bf16[36,72,128]{2,1,0:T(8,128)(2,1)S(1)}, bf16[36,72,128]{2,1,0:T(8,128)(2,1)S(1)}, u32[]{:S(2)}, u32[]{:S(2)}) collective-permute-start(bf16[36,72,128]{2,1,0:T(8,128)(2,1)S(1)} %collective-permute-done.1.refs_1_), channel_id=1, source_target_pairs={{0,8},{1,9},{2,10},{3,11},{4,12},{5,13},{6,14},{7,15},{16,24},{17,... | collective-permute-start | bytes 1990664 | tf_op jit(solution)/shard_map/ppermute | solution.py:375
  37.4 3.5 %solve.7.refs_9_ = f32[48,72,128]{2,1,0:T(8,128)S(1)} custom-call(bf16[48,72,128]{2,1,0:T(8,128)(2,1)S(1)} %get-tuple-element.11.refs_0_, bf16[36,72,128]{2,1,0:T(8,128)(2,1)S(1)} %get-tuple-element.12.refs_1_, f32[1776,128]{1,0:T(8,128)S(1)} %get-tuple-element.13.refs_2_.refs_3_, bf16[72,240]{1,0:T(8,128)(2,1)S(1)} %copy-done.3, ...), custom_call_target="tpu_custom_call" | custom-call | flops 2000000000 | bytes 4000000 | tf_op jit(solution)/shard_map/solve/pallas_call | solution.py:306
  41.0 3.6 %solve.8.refs_9_ = f32[48,72,128]{2,1,0:T(8,128)S(1)} custom-call(bf16[48,72,128]{2,1,0:T(8,128)(2,1)S(1)} %get-tuple-element.11.refs_0_, bf16[36,72,128]{2,1,0:T(8,128)(2,1)S(1)} %collective-permute-done.4.refs_1_, f32[1776,128]{1,0:T(8,128)S(1)} %get-tuple-element.13.refs_2_.refs_3_, bf16[72,240]{1,0:T(8,128)(2,1)S(1)} %copy-done.3, ...), custom_call_target="tpu_custom_call" | custom-call | flops 2000000000 | bytes 4000000 | tf_op jit(solution)/shard_map/solve/pallas_call | solution.py:306
  44.5 3.5 %solve.9.refs_10_ = f32[48,72,128]{2,1,0:T(8,128)S(1)} custom-call(bf16[48,72,128]{2,1,0:T(8,128)(2,1)S(1)} %get-tuple-element.11.refs_0_, bf16[36,72,128]{2,1,0:T(8,128)(2,1)S(1)} %collective-permute-done.1.refs_1_, f32[1776,128]{1,0:T(8,128)S(1)} %get-tuple-element.13.refs_2_.refs_3_, bf16[72,240]{1,0:T(8,128)(2,1)S(1)} %copy-done.3, ...), custom_call_target="tpu_custom_call" | custom-call | flops 2000000000 | bytes 4000000 | tf_op jit(solution)/shard_map/solve/pallas_call | solution.py:306
  48.1 0.0 collective-permute-done.3.refs_1_
  48.1 0.0 collective-permute-done.5.refs_2_
  48.1 3.8 %solve.10.refs_10_ = f32[48,72,128]{2,1,0:T(8,128)S(1)} custom-call(bf16[48,72,128]{2,1,0:T(8,128)(2,1)S(1)} %get-tuple-element.11.refs_0_, bf16[36,72,128]{2,1,0:T(8,128)(2,1)S(1)} %collective-permute-done.3.refs_1_, bf16[36,72,128]{2,1,0:T(8,128)(2,1)S(1)} %collective-permute-done.5.refs_2_, f32[1776,128]{1,0:T(8,128)S(1)} %get-tuple-element.13.refs_2_.refs_3_, ...), custom_call_target="tpu_custom_call" | custom-call | flops 2000000000 | bytes 4000000 | tf_op jit(solution)/shard_map/solve/pallas_call | solution.py:306
  51.9 0.0 collective-permute-done.refs_1_
  51.9 0.0 collective-permute-done.2.refs_2_
  52.0 4.2 %solve.11 = f32[8,336,128]{2,1,0:T(8,128)S(1)} custom-call(bf16[48,72,128]{2,1,0:T(8,128)(2,1)S(1)} %get-tuple-element.11.refs_0_, bf16[36,72,128]{2,1,0:T(8,128)(2,1)S(1)} %collective-permute-done.refs_1_, bf16[36,72,128]{2,1,0:T(8,128)(2,1)S(1)} %collective-permute-done.2.refs_2_, f32[1776,128]{1,0:T(8,128)S(1)} %get-tuple-element.13.refs_2_.refs_3_, ...), custom_call_target="tpu_custom_call" | custom-call | flops 2000000000 | bytes 4000000 | tf_op jit(solution)/shard_map/solve/pallas_call | solution.py:306
  56.1 0.1 convert_element_type.6
  56.2 14.4 %all_to_all.5 = f16[8,336,128]{2,1,0:T(8,128)(2,1)S(1)} all-to-all(f16[8,336,128]{2,1,0:T(8,128)(2,1)S(1)} %convert_element_type.6), channel_id=1, replica_groups=mesh['blk'=32,'col'=8] {'col'}, dimensions={0} | all-to-all | bytes 1376256 | tf_op jit(solution)/shard_map/all_to_all | solution.py:391
  70.7 0.1 convert_element_type.7
  70.8 0.1 fusion.2
  70.9 0.2 fusion.total_ref
  71.1 0.8 %gather.1 = f32[1,6,72,96]{3,2,1,0:T(8,128)} custom-call(f32[328,128]{1,0:T(8,128)S(1)} %fusion.total_ref), custom_call_target="tpu_custom_call" | custom-call | tf_op jit(solution)/shard_map/gather/pallas_call | solution.py:344
Async XLA Ops:
  0.0 23.0 %copy-start.3 = (bf16[72,240]{1,0:T(8,128)(2,1)S(1)}, bf16[72,240]{1,0:T(8,128)(2,1)}, u32[]{:S(2)}) copy-start(bf16[72,240]{1,0:T(8,128)(2,1)} %constant.19.clone.refs_3_.refs_4_) | copy-start | bytes 103684
  0.0 23.0 %copy-start.5 = (bf16[48,144]{1,0:T(8,128)(2,1)S(1)}, bf16[48,144]{1,0:T(8,128)(2,1)}, u32[]{:S(2)}) copy-start(bf16[48,144]{1,0:T(8,128)(2,1)} %constant.20.clone.refs_4_.refs_5_) | copy-start | bytes 41476
  0.0 23.0 %copy-start.1 = (bf16[256,256]{1,0:T(8,128)(2,1)S(1)}, bf16[256,256]{1,0:T(8,128)(2,1)}, u32[]{:S(2)}) copy-start(bf16[256,256]{1,0:T(8,128)(2,1)} %constant.21.clone.refs_5_.refs_6_) | copy-start | bytes 393220
  0.0 23.1 %copy-start.2 = (bf16[256,256]{1,0:T(8,128)(2,1)S(1)}, bf16[256,256]{1,0:T(8,128)(2,1)}, u32[]{:S(2)}) copy-start(bf16[256,256]{1,0:T(8,128)(2,1)} %constant.22.clone.refs_6_.refs_7_) | copy-start | bytes 393220
  0.0 23.0 %copy-start.6 = (bf16[48,144]{1,0:T(8,128)(2,1)S(1)}, bf16[48,144]{1,0:T(8,128)(2,1)}, u32[]{:S(2)}) copy-start(bf16[48,144]{1,0:T(8,128)(2,1)} %constant.23.clone.refs_7_.refs_8_) | copy-start | bytes 41476
  0.0 23.0 %copy-start.4 = (bf16[72,240]{1,0:T(8,128)(2,1)S(1)}, bf16[72,240]{1,0:T(8,128)(2,1)}, u32[]{:S(2)}) copy-start(bf16[72,240]{1,0:T(8,128)(2,1)} %constant.24.clone.refs_8_.refs_9_) | copy-start | bytes 103684
  0.0 23.0 %copy-start = (bf16[1,48,72,96]{3,2,1,0:T(8,128)(2,1)S(1)}, bf16[1,48,72,96]{3,2,1,0:T(8,128)(2,1)}, u32[]{:S(2)}) copy-start(bf16[1,48,72,96]{3,2,1,0:T(8,128)(2,1)} %refs_0_.1) | copy-start | bytes 1990660
  2.8 18.9 %collective-permute-start.4 = (bf16[36,72,128]{2,1,0:T(8,128)(2,1)S(1)}, bf16[36,72,128]{2,1,0:T(8,128)(2,1)S(1)}, u32[]{:S(2)}, u32[]{:S(2)}) collective-permute-start(bf16[36,72,128]{2,1,0:T(8,128)(2,1)S(1)} %get-tuple-element.10.refs_1_), channel_id=1, source_target_pairs={{0,8},{1,9},{2,10},{3,11},{4,12},{5,13},{6,14},{7,15},{8,17},{9,16... | collective-permute-start | bytes 1990664 | tf_op jit(solution)/shard_map/ppermute | solution.py:375
  2.9 33.0 %collective-permute-start.1 = (bf16[36,72,128]{2,1,0:T(8,128)(2,1)S(1)}, bf16[36,72,128]{2,1,0:T(8,128)(2,1)S(1)}, u32[]{:S(2)}, u32[]{:S(2)}) collective-permute-start(bf16[36,72,128]{2,1,0:T(8,128)(2,1)S(1)} %get-tuple-element.12.refs_1_), channel_id=1, source_target_pairs={{0,8},{1,9},{2,10},{3,11},{4,12},{5,13},{6,14},{7,15},{8,17},{9,16... | collective-permute-start | bytes 1990664 | tf_op jit(solution)/shard_map/ppermute | solution.py:375
  4.5 43.6 %collective-permute-start.3 = (bf16[36,72,128]{2,1,0:T(8,128)(2,1)S(1)}, bf16[36,72,128]{2,1,0:T(8,128)(2,1)S(1)}, u32[]{:S(2)}, u32[]{:S(2)}) collective-permute-start(bf16[36,72,128]{2,1,0:T(8,128)(2,1)S(1)} %get-tuple-element.10.refs_1_), channel_id=1, source_target_pairs={{0,17},{1,16},{2,19},{3,18},{4,21},{5,20},{6,23},{7,22},{16,33},{1... | collective-permute-start | bytes 1990664 | tf_op jit(solution)/shard_map/ppermute | solution.py:375
  8.3 43.7 %collective-permute-start = (bf16[36,72,128]{2,1,0:T(8,128)(2,1)S(1)}, bf16[36,72,128]{2,1,0:T(8,128)(2,1)S(1)}, u32[]{:S(2)}, u32[]{:S(2)}) collective-permute-start(bf16[36,72,128]{2,1,0:T(8,128)(2,1)S(1)} %get-tuple-element.12.refs_1_), channel_id=1, source_target_pairs={{0,17},{1,16},{2,19},{3,18},{4,21},{5,20},{6,23},{7,22},{16,33},{1... | collective-permute-start | bytes 1990664 | tf_op jit(solution)/shard_map/ppermute | solution.py:375
  21.7 26.4 %collective-permute-start.5 = (bf16[36,72,128]{2,1,0:T(8,128)(2,1)S(1)}, bf16[36,72,128]{2,1,0:T(8,128)(2,1)S(1)}, u32[]{:S(2)}, u32[]{:S(2)}) collective-permute-start(bf16[36,72,128]{2,1,0:T(8,128)(2,1)S(1)} %collective-permute-done.4.refs_1_), channel_id=1, source_target_pairs={{0,8},{1,9},{2,10},{3,11},{4,12},{5,13},{6,14},{7,15},{16,24},{17,... | collective-permute-start | bytes 1990664 | tf_op jit(solution)/shard_map/ppermute | solution.py:375
  35.9 16.0 %collective-permute-start.2 = (bf16[36,72,128]{2,1,0:T(8,128)(2,1)S(1)}, bf16[36,72,128]{2,1,0:T(8,128)(2,1)S(1)}, u32[]{:S(2)}, u32[]{:S(2)}) collective-permute-start(bf16[36,72,128]{2,1,0:T(8,128)(2,1)S(1)} %collective-permute-done.1.refs_1_), channel_id=1, source_target_pairs={{0,8},{1,9},{2,10},{3,11},{4,12},{5,13},{6,14},{7,15},{16,24},{17,... | collective-permute-start | bytes 1990664 | tf_op jit(solution)/shard_map/ppermute | solution.py:375

commit v2 on v1

--- a/solution.py
+++ b/solution.py
@@ -131,42 +131,45 @@
     return pltpu.with_memory_space_constraint(value, pltpu.HBM)
 
 
-def pack_kernel(band_ref, occupied_ref, source_ref, first_ref, second_ref, held, in_sems):
+def pack_kernel(band_hbm, occupied_hbm, source_ref, out_ref, held, sems, band_ref, occupied_ref, *, slot):
     chunks = NX // TAIL
-    planes = [pl.ds(chunk * TAIL, TAIL) for chunk in range(chunks)]
-    order = [(slot, chunk) for slot in range(2) for chunk in (chunks - 1, *range(chunks - 1))]
+    lookups = [
+        pltpu.make_async_copy(band_hbm, band_ref, sems.at[chunks]),
+        pltpu.make_async_copy(occupied_hbm, occupied_ref, sems.at[chunks + 1]),
+    ]
+    for lookup in lookups:
+        lookup.start()
     reads = {}
-    for slot, chunk in order:
-        reads[slot, chunk] = pltpu.make_async_copy(
-            source_ref.at[slot, planes[chunk]], held.at[slot, planes[chunk]], in_sems.at[slot, chunk]
-        )
-        reads[slot, chunk].start()
+    for chunk in (chunks - 1, *range(chunks - 1)):
+        planes = pl.ds(chunk * TAIL, TAIL)
+        reads[chunk] = pltpu.make_async_copy(source_ref.at[slot, planes], held.at[planes], sems.at[chunk])
+        reads[chunk].start()
+    for lookup in lookups:
+        lookup.wait()
     lane = lane_of(NY)
-    for slot, out_ref in enumerate((first_ref, second_ref)):
-        weight = jnp.where(occupied_ref[band_ref[slot]] > 0, 1.0, 0.0).astype(F32)
-        reads[slot, chunks - 1].wait()
-        for third in range(chunks - 1):
-            reads[slot, third].wait()
-            for index in range(TAIL):
-                plane = third * TAIL + index
-                base = widened(held[slot, plane])
-                tail = pltpu.roll(widened(held[slot, BASE + index]), 96 - 32 * third, 1)
-                out_ref[plane] = (jnp.where(lane < 96, base, tail) * weight).astype(BF16)
-
-
-def packed(sources, band_of_slot, occupied):
+    weight = jnp.where(occupied_ref[band_ref[slot]] > 0, 1.0, 0.0).astype(F32)
+    reads[chunks - 1].wait()
+    for third in range(chunks - 1):
+        reads[third].wait()
+        for index in range(TAIL):
+            plane = third * TAIL + index
+            base = widened(held[plane])
+            tail = pltpu.roll(widened(held[BASE + index]), 96 - 32 * third, 1)
+            out_ref[plane] = (jnp.where(lane < 96, base, tail) * weight).astype(BF16)
+
+
+def packed(sources, slot, band_of_slot, occupied):
     anywhere = pl.BlockSpec(memory_space=pl.ANY)
-    whole = pl.BlockSpec(memory_space=pltpu.VMEM)
-    scalars = pl.BlockSpec(memory_space=pltpu.SMEM)
-    shape = jax.ShapeDtypeStruct((BASE, NY, LANES), BF16)
     return pl.pallas_call(
-        pack_kernel,
-        out_shape=(shape, shape),
-        in_specs=[scalars, scalars, anywhere],
-        out_specs=(whole, whole),
+        lambda *refs: pack_kernel(*refs, slot=slot),
+        out_shape=jax.ShapeDtypeStruct((BASE, NY, LANES), BF16),
+        in_specs=[anywhere] * 3,
+        out_specs=pl.BlockSpec(memory_space=pltpu.VMEM),
         scratch_shapes=[
-            pltpu.VMEM((2, NX, NY, NZ), BF16),
-            pltpu.SemaphoreType.DMA((2, NX // TAIL)),
+            pltpu.VMEM((NX, NY, NZ), BF16),
+            pltpu.SemaphoreType.DMA((NX // TAIL + 2,)),
+            pltpu.SMEM(band_of_slot.shape, jnp.int32),
+            pltpu.SMEM(occupied.shape, jnp.int32),
         ],
         compiler_params=pltpu.CompilerParams(vmem_limit_bytes=16 << 20),
         name="pack",
@@ -377,7 +380,9 @@
 
 def shards(targets, sources, band_of_slot, occupied):
     tables = constants()
-    own = packed(sources, band_of_slot, occupied)
+    own = []
+    for slot in range(2):
+        own.append(packed(sources, slot, band_of_slot, occupied))
     near = [sent(own[slot], next_block()) for slot in range(2)]
     far = [sent(own[slot], even_ahead()) for slot in range(2)]
     passed = [sent(near[slot], even_to_odd()) for slot in range(2)]

time: 72.2 us -> 69.2 us (0.958)
  waiting for transfers between devices: 18.8 us -> 15.7 us
    ppermute x6, waiting for transfers between devices: 18.8 us -> 15.7 us  [sent(): return lax.ppermute(value, AXES, pairs)]
    pallas_call x1 -> x2, Pallas kernels: 2.73 us -> 3.07 us  [packed(): pl.pallas_call(lambda *refs: pack_kernel(*refs, slot=slot), out_shape=jax...]
  transfers between devices with their start and end apart: 6 -> 6, of which waited for: 2 -> 2; matrix products, arithmetic and copies ran while one was open for 0% -> 0% of each run, Pallas kernels for 26% -> 29%
where the time goes in v2:
time: 69.2 us; the launch traced here: 68.9 us
  Pallas kernels  26.4 us (38%)
  waiting for transfers between devices  15.7 us (23%)
  blocking collectives  14.4 us (21%)
  starting transfers between devices  11.7 us (17%)
    pallas_call x6, Pallas kernels, solved(): pl.pallas_call(lambda *refs: solve_kernel(*refs, n_sources=len(source_lis...  22.5 us
    ppermute x6, waiting for transfers between devices, sent(): return lax.ppermute(value, AXES, pairs)  15.7 us
    all_to_all x1, blocking collectives, shards(): parts = lax.all_to_all(pieces.astype(jnp.float16), 'col', 0, 0)  14.4 us
    ppermute x6, starting transfers between devices, sent(): return lax.ppermute(value, AXES, pairs)  11.7 us
    pallas_call x2, Pallas kernels, packed(): pl.pallas_call(lambda *refs: pack_kernel(*refs, slot=slot), out_shape=jax...  3.07 us
  transfers between devices with their start and end apart: 6, of which 2 were waited for; matrix products, arithmetic and copies ran while one was open for 0% of the time, Pallas kernels for 29%

profile of v2, /device:TPU:2, one launch (start us, length us, event | category | flops | bytes accessed | tf_op | source)
XLA Modules:
  0.0 68.9 jit_solution(4235551196336781407)
XLA Ops:
  0.0 1.5 %pack.2.refs_1_ = bf16[36,72,128]{2,1,0:T(8,128)(2,1)S(1)} custom-call(s32[2]{0:T(128)} %refs_0_.5, s32[512]{0:T(512)} %refs_1_.3, bf16[2,48,72,96]{3,2,1,0:T(8,128)(2,1)} %refs_2_.4), custom_call_target="tpu_custom_call" | custom-call | tf_op jit(solution)/shard_map/pack/pallas_call | solution.py:163
  1.5 0.0 copy-start
  1.5 0.0 copy-start.1
  1.5 0.0 copy-start.2
  1.5 0.0 copy-start.3
  1.5 0.0 copy-start.4
  1.6 0.0 copy-start.5
  1.6 0.0 copy-start.6
  1.6 0.1 collective-permute-start.4
  1.7 1.6 %pack.3.refs_1_ = bf16[36,72,128]{2,1,0:T(8,128)(2,1)S(1)} custom-call(s32[2]{0:T(128)} %refs_0_.5, s32[512]{0:T(512)} %refs_1_.3, bf16[2,48,72,96]{3,2,1,0:T(8,128)(2,1)} %refs_2_.4), custom_call_target="tpu_custom_call" | custom-call | tf_op jit(solution)/shard_map/pack/pallas_call | solution.py:163
  3.3 1.6 %collective-permute-start.1 = (bf16[36,72,128]{2,1,0:T(8,128)(2,1)S(1)}, bf16[36,72,128]{2,1,0:T(8,128)(2,1)S(1)}, u32[]{:S(2)}, u32[]{:S(2)}) collective-permute-start(bf16[36,72,128]{2,1,0:T(8,128)(2,1)S(1)} %pack.3.refs_1_), channel_id=1, source_target_pairs={{0,8},{1,9},{2,10},{3,11},{4,12},{5,13},{6,14},{7,15},{8,17},{9,16... | collective-permute-start | bytes 1990664 | tf_op jit(solution)/shard_map/ppermute | solution.py:378
  4.8 3.8 %collective-permute-start.3 = (bf16[36,72,128]{2,1,0:T(8,128)(2,1)S(1)}, bf16[36,72,128]{2,1,0:T(8,128)(2,1)S(1)}, u32[]{:S(2)}, u32[]{:S(2)}) collective-permute-start(bf16[36,72,128]{2,1,0:T(8,128)(2,1)S(1)} %pack.2.refs_1_), channel_id=1, source_target_pairs={{0,17},{1,16},{2,19},{3,18},{4,21},{5,20},{6,23},{7,22},{16,33},{1... | collective-permute-start | bytes 1990664 | tf_op jit(solution)/shard_map/ppermute | solution.py:378
  8.6 3.4 %collective-permute-start = (bf16[36,72,128]{2,1,0:T(8,128)(2,1)S(1)}, bf16[36,72,128]{2,1,0:T(8,128)(2,1)S(1)}, u32[]{:S(2)}, u32[]{:S(2)}) collective-permute-start(bf16[36,72,128]{2,1,0:T(8,128)(2,1)S(1)} %pack.3.refs_1_), channel_id=1, source_target_pairs={{0,17},{1,16},{2,19},{3,18},{4,21},{5,20},{6,23},{7,22},{16,33},{1... | collective-permute-start | bytes 1990664 | tf_op jit(solution)/shard_map/ppermute | solution.py:378
  12.0 6.9 %collective-permute-done.4.refs_1_ = bf16[36,72,128]{2,1,0:T(8,128)(2,1)S(1)} collective-permute-done((bf16[36,72,128]{2,1,0:T(8,128)(2,1)S(1)}, bf16[36,72,128]{2,1,0:T(8,128)(2,1)S(1)}, u32[]{:S(2)}, u32[]{:S(2)}) %collective-permute-start.4) | collective-permute-done | bytes 663584 | tf_op jit(solution)/shard_map/ppermute | solution.py:378
  18.9 1.3 %collective-permute-start.5 = (bf16[36,72,128]{2,1,0:T(8,128)(2,1)S(1)}, bf16[36,72,128]{2,1,0:T(8,128)(2,1)S(1)}, u32[]{:S(2)}, u32[]{:S(2)}) collective-permute-start(bf16[36,72,128]{2,1,0:T(8,128)(2,1)S(1)} %collective-permute-done.4.refs_1_), channel_id=1, source_target_pairs={{0,8},{1,9},{2,10},{3,11},{4,12},{5,13},{6,14},{7,15},{16,24},{17,... | collective-permute-start | bytes 1990664 | tf_op jit(solution)/shard_map/ppermute | solution.py:378
  20.2 0.0 copy-done
  20.2 0.0 copy-done.1
  20.3 0.0 copy-done.2
  20.3 0.0 copy-done.3
  20.3 0.0 copy-done.4
  20.3 0.0 copy-done.5
  20.3 0.0 copy-done.6
  20.3 4.0 %solve.6 = (f32[48,72,128]{2,1,0:T(8,128)S(1)}, bf16[48,72,128]{2,1,0:T(8,128)(2,1)S(1)}, f32[1776,128]{1,0:T(8,128)S(1)}) custom-call(bf16[1,48,72,96]{3,2,1,0:T(8,128)(2,1)S(1)} %copy-done, bf16[36,72,128]{2,1,0:T(8,128)(2,1)S(1)} %pack.2.refs_1_, f32[1776,128]{1,0:T(8,128)} %constant.18.clone.refs_2_, bf16[72,240]{1,0:T(8,128)(2,1)S(1)} %copy-done.3, ...), custom_call_target="tpu_custom_call" | custom-call | flops 2000000000 | bytes 4000000 | tf_op jit(solution)/shard_map/solve/pallas_call | solution.py:309
  24.3 8.8 %collective-permute-done.1.refs_1_ = bf16[36,72,128]{2,1,0:T(8,128)(2,1)S(1)} collective-permute-done((bf16[36,72,128]{2,1,0:T(8,128)(2,1)S(1)}, bf16[36,72,128]{2,1,0:T(8,128)(2,1)S(1)}, u32[]{:S(2)}, u32[]{:S(2)}) %collective-permute-start.1) | collective-permute-done | bytes 663584 | tf_op jit(solution)/shard_map/ppermute | solution.py:378
  33.1 1.5 %collective-permute-start.2 = (bf16[36,72,128]{2,1,0:T(8,128)(2,1)S(1)}, bf16[36,72,128]{2,1,0:T(8,128)(2,1)S(1)}, u32[]{:S(2)}, u32[]{:S(2)}) collective-permute-start(bf16[36,72,128]{2,1,0:T(8,128)(2,1)S(1)} %collective-permute-done.1.refs_1_), channel_id=1, source_target_pairs={{0,8},{1,9},{2,10},{3,11},{4,12},{5,13},{6,14},{7,15},{16,24},{17,... | collective-permute-start | bytes 1990664 | tf_op jit(solution)/shard_map/ppermute | solution.py:378
  34.6 3.5 %solve.7.refs_9_ = f32[48,72,128]{2,1,0:T(8,128)S(1)} custom-call(bf16[48,72,128]{2,1,0:T(8,128)(2,1)S(1)} %get-tuple-element.8.refs_0_, bf16[36,72,128]{2,1,0:T(8,128)(2,1)S(1)} %pack.3.refs_1_, f32[1776,128]{1,0:T(8,128)S(1)} %get-tuple-element.9.refs_2_.refs_3_, bf16[72,240]{1,0:T(8,128)(2,1)S(1)} %copy-done.3, bf16[48,144]{1,0:T(8,128)(2,1)S(1)} %copy-done.5, ...), custom_call_target="tpu_custom_call" | custom-call | flops 2000000000 | bytes 4000000 | tf_op jit(solution)/shard_map/solve/pallas_call | solution.py:309
  38.1 3.5 %solve.8.refs_9_ = f32[48,72,128]{2,1,0:T(8,128)S(1)} custom-call(bf16[48,72,128]{2,1,0:T(8,128)(2,1)S(1)} %get-tuple-element.8.refs_0_, bf16[36,72,128]{2,1,0:T(8,128)(2,1)S(1)} %collective-permute-done.4.refs_1_, f32[1776,128]{1,0:T(8,128)S(1)} %get-tuple-element.9.refs_2_.refs_3_, bf16[72,240]{1,0:T(8,128)(2,1)S(1)} %copy-done.3, ...), custom_call_target="tpu_custom_call" | custom-call | flops 2000000000 | bytes 4000000 | tf_op jit(solution)/shard_map/solve/pallas_call | solution.py:309
  41.6 3.5 %solve.9.refs_10_ = f32[48,72,128]{2,1,0:T(8,128)S(1)} custom-call(bf16[48,72,128]{2,1,0:T(8,128)(2,1)S(1)} %get-tuple-element.8.refs_0_, bf16[36,72,128]{2,1,0:T(8,128)(2,1)S(1)} %collective-permute-done.1.refs_1_, f32[1776,128]{1,0:T(8,128)S(1)} %get-tuple-element.9.refs_2_.refs_3_, bf16[72,240]{1,0:T(8,128)(2,1)S(1)} %copy-done.3, ...), custom_call_target="tpu_custom_call" | custom-call | flops 2000000000 | bytes 4000000 | tf_op jit(solution)/shard_map/solve/pallas_call | solution.py:309
  45.1 0.0 collective-permute-done.3.refs_1_
  45.1 0.0 collective-permute-done.5.refs_2_
  45.1 3.9 %solve.10.refs_10_ = f32[48,72,128]{2,1,0:T(8,128)S(1)} custom-call(bf16[48,72,128]{2,1,0:T(8,128)(2,1)S(1)} %get-tuple-element.8.refs_0_, bf16[36,72,128]{2,1,0:T(8,128)(2,1)S(1)} %collective-permute-done.3.refs_1_, bf16[36,72,128]{2,1,0:T(8,128)(2,1)S(1)} %collective-permute-done.5.refs_2_, f32[1776,128]{1,0:T(8,128)S(1)} %get-tuple-element.9.refs_2_.refs_3_, ...), custom_call_target="tpu_custom_call" | custom-call | flops 2000000000 | bytes 4000000 | tf_op jit(solution)/shard_map/solve/pallas_call | solution.py:309
  49.1 0.0 collective-permute-done.refs_1_
  49.1 0.0 collective-permute-done.2.refs_2_
  49.1 4.1 %solve.11 = f32[8,336,128]{2,1,0:T(8,128)S(1)} custom-call(bf16[48,72,128]{2,1,0:T(8,128)(2,1)S(1)} %get-tuple-element.8.refs_0_, bf16[36,72,128]{2,1,0:T(8,128)(2,1)S(1)} %collective-permute-done.refs_1_, bf16[36,72,128]{2,1,0:T(8,128)(2,1)S(1)} %collective-permute-done.2.refs_2_, f32[1776,128]{1,0:T(8,128)S(1)} %get-tuple-element.9.refs_2_.refs_3_, ...), custom_call_target="tpu_custom_call" | custom-call | flops 2000000000 | bytes 4000000 | tf_op jit(solution)/shard_map/solve/pallas_call | solution.py:309
  53.2 0.1 convert_element_type.6
  53.3 14.4 %all_to_all.5 = f16[8,336,128]{2,1,0:T(8,128)(2,1)S(1)} all-to-all(f16[8,336,128]{2,1,0:T(8,128)(2,1)S(1)} %convert_element_type.6), channel_id=1, replica_groups=mesh['blk'=32,'col'=8] {'col'}, dimensions={0} | all-to-all | bytes 1376256 | tf_op jit(solution)/shard_map/all_to_all | solution.py:396
  67.7 0.1 convert_element_type.7
  67.8 0.1 fusion.2
  68.0 0.2 fusion.total_ref
  68.1 0.8 %gather.1 = f32[1,6,72,96]{3,2,1,0:T(8,128)} custom-call(f32[328,128]{1,0:T(8,128)S(1)} %fusion.total_ref), custom_call_target="tpu_custom_call" | custom-call | tf_op jit(solution)/shard_map/gather/pallas_call | solution.py:347
Async XLA Ops:
  1.5 18.7 %copy-start = (bf16[1,48,72,96]{3,2,1,0:T(8,128)(2,1)S(1)}, bf16[1,48,72,96]{3,2,1,0:T(8,128)(2,1)}, u32[]{:S(2)}) copy-start(bf16[1,48,72,96]{3,2,1,0:T(8,128)(2,1)} %refs_0_.4) | copy-start | bytes 1990660
  1.5 18.7 %copy-start.1 = (bf16[256,256]{1,0:T(8,128)(2,1)S(1)}, bf16[256,256]{1,0:T(8,128)(2,1)}, u32[]{:S(2)}) copy-start(bf16[256,256]{1,0:T(8,128)(2,1)} %constant.21.clone.refs_5_.refs_6_) | copy-start | bytes 393220
  1.5 18.7 %copy-start.2 = (bf16[256,256]{1,0:T(8,128)(2,1)S(1)}, bf16[256,256]{1,0:T(8,128)(2,1)}, u32[]{:S(2)}) copy-start(bf16[256,256]{1,0:T(8,128)(2,1)} %constant.22.clone.refs_6_.refs_7_) | copy-start | bytes 393220
  1.5 18.7 %copy-start.3 = (bf16[72,240]{1,0:T(8,128)(2,1)S(1)}, bf16[72,240]{1,0:T(8,128)(2,1)}, u32[]{:S(2)}) copy-start(bf16[72,240]{1,0:T(8,128)(2,1)} %constant.19.clone.refs_3_.refs_4_) | copy-start | bytes 103684
  1.5 18.7 %copy-start.4 = (bf16[72,240]{1,0:T(8,128)(2,1)S(1)}, bf16[72,240]{1,0:T(8,128)(2,1)}, u32[]{:S(2)}) copy-start(bf16[72,240]{1,0:T(8,128)(2,1)} %constant.24.clone.refs_8_.refs_9_) | copy-start | bytes 103684
  1.6 18.7 %copy-start.5 = (bf16[48,144]{1,0:T(8,128)(2,1)S(1)}, bf16[48,144]{1,0:T(8,128)(2,1)}, u32[]{:S(2)}) copy-start(bf16[48,144]{1,0:T(8,128)(2,1)} %constant.20.clone.refs_4_.refs_5_) | copy-start | bytes 41476
  1.6 18.7 %copy-start.6 = (bf16[48,144]{1,0:T(8,128)(2,1)S(1)}, bf16[48,144]{1,0:T(8,128)(2,1)}, u32[]{:S(2)}) copy-start(bf16[48,144]{1,0:T(8,128)(2,1)} %constant.23.clone.refs_7_.refs_8_) | copy-start | bytes 41476
  1.6 17.3 %collective-permute-start.4 = (bf16[36,72,128]{2,1,0:T(8,128)(2,1)S(1)}, bf16[36,72,128]{2,1,0:T(8,128)(2,1)S(1)}, u32[]{:S(2)}, u32[]{:S(2)}) collective-permute-start(bf16[36,72,128]{2,1,0:T(8,128)(2,1)S(1)} %pack.2.refs_1_), channel_id=1, source_target_pairs={{0,8},{1,9},{2,10},{3,11},{4,12},{5,13},{6,14},{7,15},{8,17},{9,16... | collective-permute-start | bytes 1990664 | tf_op jit(solution)/shard_map/ppermute | solution.py:378
  3.3 29.9 %collective-permute-start.1 = (bf16[36,72,128]{2,1,0:T(8,128)(2,1)S(1)}, bf16[36,72,128]{2,1,0:T(8,128)(2,1)S(1)}, u32[]{:S(2)}, u32[]{:S(2)}) collective-permute-start(bf16[36,72,128]{2,1,0:T(8,128)(2,1)S(1)} %pack.3.refs_1_), channel_id=1, source_target_pairs={{0,8},{1,9},{2,10},{3,11},{4,12},{5,13},{6,14},{7,15},{8,17},{9,16... | collective-permute-start | bytes 1990664 | tf_op jit(solution)/shard_map/ppermute | solution.py:378
  4.8 40.3 %collective-permute-start.3 = (bf16[36,72,128]{2,1,0:T(8,128)(2,1)S(1)}, bf16[36,72,128]{2,1,0:T(8,128)(2,1)S(1)}, u32[]{:S(2)}, u32[]{:S(2)}) collective-permute-start(bf16[36,72,128]{2,1,0:T(8,128)(2,1)S(1)} %pack.2.refs_1_), channel_id=1, source_target_pairs={{0,17},{1,16},{2,19},{3,18},{4,21},{5,20},{6,23},{7,22},{16,33},{1... | collective-permute-start | bytes 1990664 | tf_op jit(solution)/shard_map/ppermute | solution.py:378
  8.6 40.4 %collective-permute-start = (bf16[36,72,128]{2,1,0:T(8,128)(2,1)S(1)}, bf16[36,72,128]{2,1,0:T(8,128)(2,1)S(1)}, u32[]{:S(2)}, u32[]{:S(2)}) collective-permute-start(bf16[36,72,128]{2,1,0:T(8,128)(2,1)S(1)} %pack.3.refs_1_), channel_id=1, source_target_pairs={{0,17},{1,16},{2,19},{3,18},{4,21},{5,20},{6,23},{7,22},{16,33},{1... | collective-permute-start | bytes 1990664 | tf_op jit(solution)/shard_map/ppermute | solution.py:378
  18.9 26.2 %collective-permute-start.5 = (bf16[36,72,128]{2,1,0:T(8,128)(2,1)S(1)}, bf16[36,72,128]{2,1,0:T(8,128)(2,1)S(1)}, u32[]{:S(2)}, u32[]{:S(2)}) collective-permute-start(bf16[36,72,128]{2,1,0:T(8,128)(2,1)S(1)} %collective-permute-done.4.refs_1_), channel_id=1, source_target_pairs={{0,8},{1,9},{2,10},{3,11},{4,12},{5,13},{6,14},{7,15},{16,24},{17,... | collective-permute-start | bytes 1990664 | tf_op jit(solution)/shard_map/ppermute | solution.py:378
  33.1 16.0 %collective-permute-start.2 = (bf16[36,72,128]{2,1,0:T(8,128)(2,1)S(1)}, bf16[36,72,128]{2,1,0:T(8,128)(2,1)S(1)}, u32[]{:S(2)}, u32[]{:S(2)}) collective-permute-start(bf16[36,72,128]{2,1,0:T(8,128)(2,1)S(1)} %collective-permute-done.1.refs_1_), channel_id=1, source_target_pairs={{0,8},{1,9},{2,10},{3,11},{4,12},{5,13},{6,14},{7,15},{16,24},{17,... | collective-permute-start | bytes 1990664 | tf_op jit(solution)/shard_map/ppermute | solution.py:378

commit v3 on v2

--- a/solution.py
+++ b/solution.py
@@ -219,7 +219,10 @@
     lane = lane_of(NY)
 
     def held_plane(plane):
-        return sum(ref[plane].astype(F32) for ref in source_refs)
+        value = source_refs[0][plane]
+        for ref in source_refs[1:]:
+            value = value + ref[plane]
+        return value.astype(F32)
 
     def first_plane(plane):
         if plane < BASE:
@@ -342,8 +345,8 @@
 
 def gathered(parts):
     whole = pl.BlockSpec(memory_space=pltpu.VMEM)
-    wide = parts.astype(F32)
-    total = jnp.sum(wide[:, : 8 * KEPT] * jnp.exp2(wide[:, 8 * KEPT : 8 * KEPT + 1, :1]), axis=0)
+    scale = jnp.exp2(parts[:, 8 * KEPT : 8 * KEPT + 1, :1].astype(F32))
+    total = jnp.sum(parts[:, : 8 * KEPT].astype(F32) * scale, axis=0)
     return pl.pallas_call(
         gather_kernel,
         out_shape=jax.ShapeDtypeStruct((1, SLICE, NY, NZ), F32),

time: 69.2 us -> 69.1 us (level)
  no operation moved by 1% of the time
where the time goes in v3:
time: 69.1 us; the launch traced here: 68.8 us
  Pallas kernels  26.4 us (38%)
  waiting for transfers between devices  15.7 us (23%)
  blocking collectives  14.4 us (21%)
  starting transfers between devices  11.7 us (17%)
    pallas_call x6, Pallas kernels, solved(): pl.pallas_call(lambda *refs: solve_kernel(*refs, n_sources=len(source_lis...  22.5 us
    ppermute x6, waiting for transfers between devices, sent(): return lax.ppermute(value, AXES, pairs)  15.7 us
    all_to_all x1, blocking collectives, shards(): parts = lax.all_to_all(pieces.astype(jnp.float16), 'col', 0, 0)  14.4 us
    ppermute x6, starting transfers between devices, sent(): return lax.ppermute(value, AXES, pairs)  11.7 us
    pallas_call x2, Pallas kernels, packed(): pl.pallas_call(lambda *refs: pack_kernel(*refs, slot=slot), out_shape=jax...  3.07 us
  transfers between devices with their start and end apart: 6, of which 2 were waited for; matrix products, arithmetic and copies ran while one was open for 0% of the time, Pallas kernels for 29%

profile of v3, /device:TPU:2, one launch (start us, length us, event | category | flops | bytes accessed | tf_op | source)
XLA Modules:
  0.0 68.8 jit_solution(500147410452281721)
XLA Ops:
  0.0 1.5 %pack.2.refs_1_ = bf16[36,72,128]{2,1,0:T(8,128)(2,1)S(1)} custom-call(s32[2]{0:T(128)} %refs_0_.5, s32[512]{0:T(512)} %refs_1_.3, bf16[2,48,72,96]{3,2,1,0:T(8,128)(2,1)} %refs_2_.4), custom_call_target="tpu_custom_call" | custom-call | tf_op jit(solution)/shard_map/pack/pallas_call | solution.py:163
  1.5 0.0 copy-start
  1.5 0.0 copy-start.1
  1.5 0.0 copy-start.2
  1.5 0.0 copy-start.3
  1.5 0.0 copy-start.4
  1.6 0.0 copy-start.5
  1.6 0.0 copy-start.6
  1.6 0.1 collective-permute-start.4
  1.7 1.6 %pack.3.refs_1_ = bf16[36,72,128]{2,1,0:T(8,128)(2,1)S(1)} custom-call(s32[2]{0:T(128)} %refs_0_.5, s32[512]{0:T(512)} %refs_1_.3, bf16[2,48,72,96]{3,2,1,0:T(8,128)(2,1)} %refs_2_.4), custom_call_target="tpu_custom_call" | custom-call | tf_op jit(solution)/shard_map/pack/pallas_call | solution.py:163
  3.3 1.6 %collective-permute-start.1 = (bf16[36,72,128]{2,1,0:T(8,128)(2,1)S(1)}, bf16[36,72,128]{2,1,0:T(8,128)(2,1)S(1)}, u32[]{:S(2)}, u32[]{:S(2)}) collective-permute-start(bf16[36,72,128]{2,1,0:T(8,128)(2,1)S(1)} %pack.3.refs_1_), channel_id=1, source_target_pairs={{0,8},{1,9},{2,10},{3,11},{4,12},{5,13},{6,14},{7,15},{8,17},{9,16... | collective-permute-start | bytes 1990664 | tf_op jit(solution)/shard_map/ppermute | solution.py:381
  4.8 3.8 %collective-permute-start.3 = (bf16[36,72,128]{2,1,0:T(8,128)(2,1)S(1)}, bf16[36,72,128]{2,1,0:T(8,128)(2,1)S(1)}, u32[]{:S(2)}, u32[]{:S(2)}) collective-permute-start(bf16[36,72,128]{2,1,0:T(8,128)(2,1)S(1)} %pack.2.refs_1_), channel_id=1, source_target_pairs={{0,17},{1,16},{2,19},{3,18},{4,21},{5,20},{6,23},{7,22},{16,33},{1... | collective-permute-start | bytes 1990664 | tf_op jit(solution)/shard_map/ppermute | solution.py:381
  8.6 3.4 %collective-permute-start = (bf16[36,72,128]{2,1,0:T(8,128)(2,1)S(1)}, bf16[36,72,128]{2,1,0:T(8,128)(2,1)S(1)}, u32[]{:S(2)}, u32[]{:S(2)}) collective-permute-start(bf16[36,72,128]{2,1,0:T(8,128)(2,1)S(1)} %pack.3.refs_1_), channel_id=1, source_target_pairs={{0,17},{1,16},{2,19},{3,18},{4,21},{5,20},{6,23},{7,22},{16,33},{1... | collective-permute-start | bytes 1990664 | tf_op jit(solution)/shard_map/ppermute | solution.py:381
  12.0 6.9 %collective-permute-done.4.refs_1_ = bf16[36,72,128]{2,1,0:T(8,128)(2,1)S(1)} collective-permute-done((bf16[36,72,128]{2,1,0:T(8,128)(2,1)S(1)}, bf16[36,72,128]{2,1,0:T(8,128)(2,1)S(1)}, u32[]{:S(2)}, u32[]{:S(2)}) %collective-permute-start.4) | collective-permute-done | bytes 663584 | tf_op jit(solution)/shard_map/ppermute | solution.py:381
  18.9 1.3 %collective-permute-start.5 = (bf16[36,72,128]{2,1,0:T(8,128)(2,1)S(1)}, bf16[36,72,128]{2,1,0:T(8,128)(2,1)S(1)}, u32[]{:S(2)}, u32[]{:S(2)}) collective-permute-start(bf16[36,72,128]{2,1,0:T(8,128)(2,1)S(1)} %collective-permute-done.4.refs_1_), channel_id=1, source_target_pairs={{0,8},{1,9},{2,10},{3,11},{4,12},{5,13},{6,14},{7,15},{16,24},{17,... | collective-permute-start | bytes 1990664 | tf_op jit(solution)/shard_map/ppermute | solution.py:381
  20.2 0.0 copy-done
  20.2 0.0 copy-done.1
  20.3 0.0 copy-done.2
  20.3 0.0 copy-done.3
  20.3 0.0 copy-done.4
  20.3 0.0 copy-done.5
  20.3 0.0 copy-done.6
  20.3 4.0 %solve.6 = (f32[48,72,128]{2,1,0:T(8,128)S(1)}, bf16[48,72,128]{2,1,0:T(8,128)(2,1)S(1)}, f32[1776,128]{1,0:T(8,128)S(1)}) custom-call(bf16[1,48,72,96]{3,2,1,0:T(8,128)(2,1)S(1)} %copy-done, bf16[36,72,128]{2,1,0:T(8,128)(2,1)S(1)} %pack.2.refs_1_, f32[1776,128]{1,0:T(8,128)} %constant.18.clone.refs_2_, bf16[72,240]{1,0:T(8,128)(2,1)S(1)} %copy-done.3, ...), custom_call_target="tpu_custom_call" | custom-call | flops 2000000000 | bytes 4000000 | tf_op jit(solution)/shard_map/solve/pallas_call | solution.py:312
  24.3 8.8 %collective-permute-done.1.refs_1_ = bf16[36,72,128]{2,1,0:T(8,128)(2,1)S(1)} collective-permute-done((bf16[36,72,128]{2,1,0:T(8,128)(2,1)S(1)}, bf16[36,72,128]{2,1,0:T(8,128)(2,1)S(1)}, u32[]{:S(2)}, u32[]{:S(2)}) %collective-permute-start.1) | collective-permute-done | bytes 663584 | tf_op jit(solution)/shard_map/ppermute | solution.py:381
  33.1 1.5 %collective-permute-start.2 = (bf16[36,72,128]{2,1,0:T(8,128)(2,1)S(1)}, bf16[36,72,128]{2,1,0:T(8,128)(2,1)S(1)}, u32[]{:S(2)}, u32[]{:S(2)}) collective-permute-start(bf16[36,72,128]{2,1,0:T(8,128)(2,1)S(1)} %collective-permute-done.1.refs_1_), channel_id=1, source_target_pairs={{0,8},{1,9},{2,10},{3,11},{4,12},{5,13},{6,14},{7,15},{16,24},{17,... | collective-permute-start | bytes 1990664 | tf_op jit(solution)/shard_map/ppermute | solution.py:381
  34.6 3.5 %solve.7.refs_9_ = f32[48,72,128]{2,1,0:T(8,128)S(1)} custom-call(bf16[48,72,128]{2,1,0:T(8,128)(2,1)S(1)} %get-tuple-element.8.refs_0_, bf16[36,72,128]{2,1,0:T(8,128)(2,1)S(1)} %pack.3.refs_1_, f32[1776,128]{1,0:T(8,128)S(1)} %get-tuple-element.9.refs_2_.refs_3_, bf16[72,240]{1,0:T(8,128)(2,1)S(1)} %copy-done.3, bf16[48,144]{1,0:T(8,128)(2,1)S(1)} %copy-done.5, ...), custom_call_target="tpu_custom_call" | custom-call | flops 2000000000 | bytes 4000000 | tf_op jit(solution)/shard_map/solve/pallas_call | solution.py:312
  38.1 3.5 %solve.8.refs_9_ = f32[48,72,128]{2,1,0:T(8,128)S(1)} custom-call(bf16[48,72,128]{2,1,0:T(8,128)(2,1)S(1)} %get-tuple-element.8.refs_0_, bf16[36,72,128]{2,1,0:T(8,128)(2,1)S(1)} %collective-permute-done.4.refs_1_, f32[1776,128]{1,0:T(8,128)S(1)} %get-tuple-element.9.refs_2_.refs_3_, bf16[72,240]{1,0:T(8,128)(2,1)S(1)} %copy-done.3, ...), custom_call_target="tpu_custom_call" | custom-call | flops 2000000000 | bytes 4000000 | tf_op jit(solution)/shard_map/solve/pallas_call | solution.py:312
  41.6 3.5 %solve.9.refs_10_ = f32[48,72,128]{2,1,0:T(8,128)S(1)} custom-call(bf16[48,72,128]{2,1,0:T(8,128)(2,1)S(1)} %get-tuple-element.8.refs_0_, bf16[36,72,128]{2,1,0:T(8,128)(2,1)S(1)} %collective-permute-done.1.refs_1_, f32[1776,128]{1,0:T(8,128)S(1)} %get-tuple-element.9.refs_2_.refs_3_, bf16[72,240]{1,0:T(8,128)(2,1)S(1)} %copy-done.3, ...), custom_call_target="tpu_custom_call" | custom-call | flops 2000000000 | bytes 4000000 | tf_op jit(solution)/shard_map/solve/pallas_call | solution.py:312
  45.1 0.0 collective-permute-done.3.refs_1_
  45.1 0.0 collective-permute-done.5.refs_2_
  45.1 3.9 %solve.10.refs_10_ = f32[48,72,128]{2,1,0:T(8,128)S(1)} custom-call(bf16[48,72,128]{2,1,0:T(8,128)(2,1)S(1)} %get-tuple-element.8.refs_0_, bf16[36,72,128]{2,1,0:T(8,128)(2,1)S(1)} %collective-permute-done.3.refs_1_, bf16[36,72,128]{2,1,0:T(8,128)(2,1)S(1)} %collective-permute-done.5.refs_2_, f32[1776,128]{1,0:T(8,128)S(1)} %get-tuple-element.9.refs_2_.refs_3_, ...), custom_call_target="tpu_custom_call" | custom-call | flops 2000000000 | bytes 4000000 | tf_op jit(solution)/shard_map/solve/pallas_call | solution.py:312
  49.0 0.0 collective-permute-done.refs_1_
  49.0 0.0 collective-permute-done.2.refs_2_
  49.1 4.1 %solve.11 = f32[8,336,128]{2,1,0:T(8,128)S(1)} custom-call(bf16[48,72,128]{2,1,0:T(8,128)(2,1)S(1)} %get-tuple-element.8.refs_0_, bf16[36,72,128]{2,1,0:T(8,128)(2,1)S(1)} %collective-permute-done.refs_1_, bf16[36,72,128]{2,1,0:T(8,128)(2,1)S(1)} %collective-permute-done.2.refs_2_, f32[1776,128]{1,0:T(8,128)S(1)} %get-tuple-element.9.refs_2_.refs_3_, ...), custom_call_target="tpu_custom_call" | custom-call | flops 2000000000 | bytes 4000000 | tf_op jit(solution)/shard_map/solve/pallas_call | solution.py:312
  53.1 0.1 convert_element_type.9
  53.2 14.4 %all_to_all.5 = f16[8,336,128]{2,1,0:T(8,128)(2,1)S(1)} all-to-all(f16[8,336,128]{2,1,0:T(8,128)(2,1)S(1)} %convert_element_type.9), channel_id=1, replica_groups=mesh['blk'=32,'col'=8] {'col'}, dimensions={0} | all-to-all | bytes 1376256 | tf_op jit(solution)/shard_map/all_to_all | solution.py:399
  67.7 0.1 fusion.2
  67.8 0.2 multiply_reduce_fusion.total_ref
  68.0 0.8 %gather.1 = f32[1,6,72,96]{3,2,1,0:T(8,128)} custom-call(f32[328,128]{1,0:T(8,128)S(1)} %multiply_reduce_fusion.total_ref), custom_call_target="tpu_custom_call" | custom-call | tf_op jit(solution)/shard_map/gather/pallas_call | solution.py:350
Async XLA Ops:
  1.5 18.7 %copy-start = (bf16[1,48,72,96]{3,2,1,0:T(8,128)(2,1)S(1)}, bf16[1,48,72,96]{3,2,1,0:T(8,128)(2,1)}, u32[]{:S(2)}) copy-start(bf16[1,48,72,96]{3,2,1,0:T(8,128)(2,1)} %refs_0_.4) | copy-start | bytes 1990660
  1.5 18.7 %copy-start.1 = (bf16[256,256]{1,0:T(8,128)(2,1)S(1)}, bf16[256,256]{1,0:T(8,128)(2,1)}, u32[]{:S(2)}) copy-start(bf16[256,256]{1,0:T(8,128)(2,1)} %constant.21.clone.refs_5_.refs_6_) | copy-start | bytes 393220
  1.5 18.7 %copy-start.2 = (bf16[256,256]{1,0:T(8,128)(2,1)S(1)}, bf16[256,256]{1,0:T(8,128)(2,1)}, u32[]{:S(2)}) copy-start(bf16[256,256]{1,0:T(8,128)(2,1)} %constant.22.clone.refs_6_.refs_7_) | copy-start | bytes 393220
  1.5 18.7 %copy-start.3 = (bf16[72,240]{1,0:T(8,128)(2,1)S(1)}, bf16[72,240]{1,0:T(8,128)(2,1)}, u32[]{:S(2)}) copy-start(bf16[72,240]{1,0:T(8,128)(2,1)} %constant.19.clone.refs_3_.refs_4_) | copy-start | bytes 103684
  1.5 18.7 %copy-start.4 = (bf16[72,240]{1,0:T(8,128)(2,1)S(1)}, bf16[72,240]{1,0:T(8,128)(2,1)}, u32[]{:S(2)}) copy-start(bf16[72,240]{1,0:T(8,128)(2,1)} %constant.24.clone.refs_8_.refs_9_) | copy-start | bytes 103684
  1.6 18.7 %copy-start.5 = (bf16[48,144]{1,0:T(8,128)(2,1)S(1)}, bf16[48,144]{1,0:T(8,128)(2,1)}, u32[]{:S(2)}) copy-start(bf16[48,144]{1,0:T(8,128)(2,1)} %constant.20.clone.refs_4_.refs_5_) | copy-start | bytes 41476
  1.6 18.7 %copy-start.6 = (bf16[48,144]{1,0:T(8,128)(2,1)S(1)}, bf16[48,144]{1,0:T(8,128)(2,1)}, u32[]{:S(2)}) copy-start(bf16[48,144]{1,0:T(8,128)(2,1)} %constant.23.clone.refs_7_.refs_8_) | copy-start | bytes 41476
  1.6 17.3 %collective-permute-start.4 = (bf16[36,72,128]{2,1,0:T(8,128)(2,1)S(1)}, bf16[36,72,128]{2,1,0:T(8,128)(2,1)S(1)}, u32[]{:S(2)}, u32[]{:S(2)}) collective-permute-start(bf16[36,72,128]{2,1,0:T(8,128)(2,1)S(1)} %pack.2.refs_1_), channel_id=1, source_target_pairs={{0,8},{1,9},{2,10},{3,11},{4,12},{5,13},{6,14},{7,15},{8,17},{9,16... | collective-permute-start | bytes 1990664 | tf_op jit(solution)/shard_map/ppermute | solution.py:381
  3.3 29.9 %collective-permute-start.1 = (bf16[36,72,128]{2,1,0:T(8,128)(2,1)S(1)}, bf16[36,72,128]{2,1,0:T(8,128)(2,1)S(1)}, u32[]{:S(2)}, u32[]{:S(2)}) collective-permute-start(bf16[36,72,128]{2,1,0:T(8,128)(2,1)S(1)} %pack.3.refs_1_), channel_id=1, source_target_pairs={{0,8},{1,9},{2,10},{3,11},{4,12},{5,13},{6,14},{7,15},{8,17},{9,16... | collective-permute-start | bytes 1990664 | tf_op jit(solution)/shard_map/ppermute | solution.py:381
  4.8 40.3 %collective-permute-start.3 = (bf16[36,72,128]{2,1,0:T(8,128)(2,1)S(1)}, bf16[36,72,128]{2,1,0:T(8,128)(2,1)S(1)}, u32[]{:S(2)}, u32[]{:S(2)}) collective-permute-start(bf16[36,72,128]{2,1,0:T(8,128)(2,1)S(1)} %pack.2.refs_1_), channel_id=1, source_target_pairs={{0,17},{1,16},{2,19},{3,18},{4,21},{5,20},{6,23},{7,22},{16,33},{1... | collective-permute-start | bytes 1990664 | tf_op jit(solution)/shard_map/ppermute | solution.py:381
  8.6 40.4 %collective-permute-start = (bf16[36,72,128]{2,1,0:T(8,128)(2,1)S(1)}, bf16[36,72,128]{2,1,0:T(8,128)(2,1)S(1)}, u32[]{:S(2)}, u32[]{:S(2)}) collective-permute-start(bf16[36,72,128]{2,1,0:T(8,128)(2,1)S(1)} %pack.3.refs_1_), channel_id=1, source_target_pairs={{0,17},{1,16},{2,19},{3,18},{4,21},{5,20},{6,23},{7,22},{16,33},{1... | collective-permute-start | bytes 1990664 | tf_op jit(solution)/shard_map/ppermute | solution.py:381
  18.9 26.2 %collective-permute-start.5 = (bf16[36,72,128]{2,1,0:T(8,128)(2,1)S(1)}, bf16[36,72,128]{2,1,0:T(8,128)(2,1)S(1)}, u32[]{:S(2)}, u32[]{:S(2)}) collective-permute-start(bf16[36,72,128]{2,1,0:T(8,128)(2,1)S(1)} %collective-permute-done.4.refs_1_), channel_id=1, source_target_pairs={{0,8},{1,9},{2,10},{3,11},{4,12},{5,13},{6,14},{7,15},{16,24},{17,... | collective-permute-start | bytes 1990664 | tf_op jit(solution)/shard_map/ppermute | solution.py:381
  33.1 15.9 %collective-permute-start.2 = (bf16[36,72,128]{2,1,0:T(8,128)(2,1)S(1)}, bf16[36,72,128]{2,1,0:T(8,128)(2,1)S(1)}, u32[]{:S(2)}, u32[]{:S(2)}) collective-permute-start(bf16[36,72,128]{2,1,0:T(8,128)(2,1)S(1)} %collective-permute-done.1.refs_1_), channel_id=1, source_target_pairs={{0,8},{1,9},{2,10},{3,11},{4,12},{5,13},{6,14},{7,15},{16,24},{17,... | collective-permute-start | bytes 1990664 | tf_op jit(solution)/shard_map/ppermute | solution.py:381
